TPU v7x, 512 devices: a whole 4x8x8 slice. The times are simulated.
512 devices in a mesh: band: 4 (over x), tile: 16 (over y_lo, z), slab: 8 (over y_hi, core).
Axes of the slice: x: 4, y: 8 (y_hi: 4, y_lo: 2; y = y_hi * 2 + y_lo), z: 8, core: 2. Of those that a mesh axis runs over, the one named last changes fastest.
Arguments:
- strength: float32 [32], P('band'), may hold values from 0.0005 to 0.5
- opacity: float32 [64, 256, 256], P('slab', 'tile'), may hold values from 0.5 to 2
- planck: float32 [64, 256, 256], P('slab', 'tile'), may hold values from 0.5 to 2
- old_populations: float32 [5, 64, 256, 256], P(None, 'slab', 'tile'), may hold values from 0.1 to 1
- line_index: int32 [32], P('band'), may hold values from 0 to 4
- line_weight: float32 [32], P('band'), may hold values from 0.2 to 1
Outputs:
- new_populations: float32 [5, 64, 256, 256], P(None, 'slab', 'tile', 'band')
- new_source: float32 [32, 64, 256, 256], P('band', 'slab', 'tile')
Inputs may be any that keep to these rules, and one draw needn't show every extreme that they name: line_index names a transition of the model atom.
All inputs are finite; a program needn't handle non-finite values.
Results may differ from a plain program's by a relative error of at most 0.0001.
Values sent between devices are 32-bit elements; how exact they have to be, the bound alone decides.
No kernel may reach another device: no remote copies, remote signals or barrier semaphores. Data moves between devices by JAX's collectives and lax.ppermute only.
A program may use at most 64 MiB of HBM per device.

v0:
```python
import jax
import jax.numpy as jnp
from jax import lax
from jax.sharding import PartitionSpec as P

LINES = 5


EPS_THERMAL = 0.1
COLLISION = 0.5
PATH_FACTOR = 1.25
TILT_SHARE = 0.4
LOWER_LEVEL = (0, 0, 1, 1, 2)
UPPER_LEVEL = (3, 4, 3, 4, 4)


def extended_2(cells, sides, width):
    for axis, dim in sides:
        count = lax.axis_size(axis)
        ends = count - 1
        head = lax.slice_in_dim(cells, 0, width, axis=dim)
        tail = lax.slice_in_dim(cells, cells.shape[dim] - width, cells.shape[dim], axis=dim)
        cells = jnp.concatenate(
            [
                lax.ppermute(tail, axis, [(i, (i + 1) % count) for i in range(ends)]),
                cells,
                lax.ppermute(head, axis, [((i + 1) % count, i) for i in range(ends)]),
            ],
            axis=dim,
        )
    return cells


def shifted(block, axis, distance):
    devices = range(lax.axis_size(axis))
    route = [(i - distance, i) for i in devices if i - distance in devices]
    return lax.ppermute(block, axis, route)


def relax(jbar, planck):
    ratios = (jbar + COLLISION * planck[None]) / (1.0 + jbar + COLLISION)
    ground = jnp.ones_like(planck)
    level_three = ratios[0]
    level_four = ratios[1]
    level_one = 0.5 * (level_three / ratios[2] + level_four / ratios[3])
    level_two = level_four / ratios[4]
    stacked = jnp.stack([ground, level_one, level_two, level_three, level_four], axis=0)
    return stacked / jnp.sum(stacked, axis=0)


def line_sources(levels_now):
    return jnp.stack(
        [
            levels_now[UPPER_LEVEL[t]] / (levels_now[LOWER_LEVEL[t]] + levels_now[UPPER_LEVEL[t]])
            for t in range(5)
        ],
        axis=0,
    )


def sweep(face_ext, strength, opacity_ext, source_ext, margin):
    intensity = face_ext
    layer_sums = []
    for plane in range(opacity_ext.shape[0]):
        attenuation = jnp.exp(-PATH_FACTOR * strength[:, None, None] * opacity_ext[plane][None])[
            :, None
        ]
        zero_column = jnp.zeros_like(intensity[:, 0, :1])
        from_left = jnp.concatenate([zero_column, intensity[:, 0, :-1]], axis=1)
        from_right = jnp.concatenate([intensity[:, 1, 1:], zero_column], axis=1)
        upwind = jnp.stack([from_left, from_right], axis=1)
        intensity = (
            attenuation * ((1.0 - TILT_SHARE) * intensity + TILT_SHARE * upwind)
            + (1.0 - attenuation) * source_ext[:, plane][:, None]
        )
        layer_sums.append(jnp.sum(intensity[:, :, margin:-margin], axis=1))
    return (intensity[:, :, margin:-margin], jnp.stack(layer_sums, axis=1))


def per_device(strength, opacity, planck, old_populations, line_index, line_weight):
    highest = lax.Precision.HIGHEST
    slab_depth, tile_rows, cells_y = opacity.shape
    freq_count = strength.shape[0]
    total_freqs = freq_count * lax.axis_size("band")
    onehot = (line_index[:, None] == jnp.arange(LINES, dtype=jnp.int32)[None, :]).astype(
        jnp.float32
    )
    weighted = onehot * line_weight[:, None] * (LINES / (2.0 * total_freqs))
    fields = jnp.concatenate([opacity[None], planck[None], old_populations], axis=0)
    fields_ext = extended_2(fields, (("tile", 2),), slab_depth)
    opacity_ext = fields_ext[0]
    planck_ext = fields_ext[1]
    levels_ext = fields_ext[2:]
    extended = tile_rows + 2 * slab_depth
    global_x = (
        lax.axis_index("tile") * tile_rows - slab_depth + jnp.arange(extended, dtype=jnp.int32)
    )
    inside = ((global_x >= 0) & (global_x < tile_rows * lax.axis_size("tile")))[None, :, None]
    lower_ext = jnp.stack([levels_ext[LOWER_LEVEL[t]] for t in range(5)], axis=0)
    upper_ext = jnp.stack([levels_ext[UPPER_LEVEL[t]] for t in range(5)], axis=0)
    denominator = jnp.where(inside, lower_ext + upper_ext, 1.0)
    line_ext = jnp.where(inside, upper_ext / denominator, 0.0)
    source_ext = jnp.where(
        inside,
        EPS_THERMAL * planck_ext[None]
        + (1.0 - EPS_THERMAL) * jnp.einsum("ft,tzxy->fzxy", onehot, line_ext, precision=highest),
        0.0,
    )
    slab_count = lax.axis_size("slab")

    def whole_step(step, carry):
        face_in, previous = carry
        face_ext = extended_2(face_in, (("tile", 2),), slab_depth)
        bottom, layer_sums = sweep(face_ext, strength, opacity_ext, source_ext, slab_depth)
        return (shifted(bottom, "slab", 1), layer_sums)

    face_start = jnp.zeros((freq_count, 2, tile_rows, cells_y), jnp.float32)
    initial = (face_start, jnp.zeros((freq_count, slab_depth, tile_rows, cells_y), jnp.float32))
    _, layer_sums = lax.fori_loop(0, slab_count, whole_step, initial)
    jbar = jnp.einsum("ft,fzxy->tzxy", weighted, layer_sums, precision=highest)
    share = cells_y // lax.axis_size("band")
    offset = lax.axis_index("band") * share
    jbar_share = lax.psum_scatter(jbar, "band", scatter_dimension=3, tiled=True)
    planck_share = lax.dynamic_slice_in_dim(planck, offset, share, 2)
    populations_share = relax(jbar_share, planck_share)
    populations_all = lax.all_gather(populations_share, "band", axis=3, tiled=True)
    new_source = EPS_THERMAL * planck[None] + (1.0 - EPS_THERMAL) * jnp.einsum(
        "ft,tzxy->fzxy", onehot, line_sources(populations_all), precision=highest
    )
    return (populations_share, new_source)


def solution(mesh):
    in_specs = (
        P("band"),
        P("slab", "tile", None),
        P("slab", "tile", None),
        P(None, "slab", "tile", None),
        P("band"),
        P("band"),
    )
    out_specs = (P(None, "slab", "tile", "band"), P("band", "slab", "tile", None))
    return jax.shard_map(
        per_device, mesh=mesh, in_specs=in_specs, out_specs=out_specs, check_vma=False
    )
```

profile of v0, /device:TPU:8, one launch (start us, length us, event | category | flops | bytes accessed | tf_op | source)
XLA Modules:
  0.0 435.0 jit_solution(6454355539191148617)
XLA Ops:
  8.7 4.3 collective-permute-start.3
  13.0 8.5 %collective-permute-start.4 = (f32[7,8,8,256]{3,2,1,0:T(8,128)S(1)}, f32[7,8,8,256]{3,2,1,0:T(8,128)}, u32[]{:S(2)}, u32[]{:S(2)}) collective-permute-start(f32[7,8,8,256]{3,2,1,0:T(8,128)S(1)} %get-tuple-element.113), channel_id=1, source_target_pairs={{8,0},{16,8},{24,16},{32,24},{40,32},{48,40},{56,48},{64,56},{72,6... | collective-permute-start | bytes 1376264 | tf_op jit(solution)/shard_map/ppermute | solution.py:27
  21.5 8.5 %collective-permute-done.3 = f32[7,8,8,256]{3,2,1,0:T(8,128)S(1)} collective-permute-done((f32[7,8,8,256]{3,2,1,0:T(8,128)S(1)}, f32[7,8,8,256]{3,2,1,0:T(8,128)S(1)}, u32[]{:S(2)}, u32[]{:S(2)}) %collective-permute-start.3) | collective-permute-done | bytes 458784 | tf_op jit(solution)/shard_map/ppermute | solution.py:25
  37.6 251.7 %while.12 = (s32[]{:T(128)}, f32[8,2,16,256]{3,2,0,1:T(8,128)S(1)}, f32[8,8,16,256]{3,2,0,1:T(8,128)}, f32[8]{0:T(128)S(1)}, f32[8,32,256]{2,1,0:T(8,128)S(1)}, /*index=5*/f32[8,8,32,256]{3,2,0,1:T(8,128)}, s32[]{:T(128)}) while((s32[]{:T(128)}, f32[8,2,16,256]{3,2,0,1:T(8,128)S(1)}, f32[8,8,16,256]{3,2,0,1:T(8,128)}, f32[8]{0:T(128)S(1)}, ...), condition=%wide.region_9.10_spmd, body=%wide.region_0.9_spmd.sunk | while | flops 24772616 | bytes 81658408 | solution.py:119
  40.5 6.6 %collective-permute-start.1 = (f32[8,2,8,256]{3,2,0,1:T(8,128)}, f32[8,2,8,256]{3,2,0,1:T(8,128)}, u32[]{:S(2)}, u32[]{:S(2)}) collective-permute-start(f32[8,2,8,256]{3,2,0,1:T(8,128)} %get-tuple-element.218), channel_id=1, source_target_pairs={{8,0},{16,8},{24,16},{32,24},{40,32},{48,40},{56,48},{64,56},{72,6... | collective-permute-start | bytes 393224 | tf_op jit(solution)/shard_map/while/body/eval_jaxpr/ppermute | solution.py:27
  67.0 6.0 %collective-permute-start.1 = (f32[8,2,8,256]{3,2,0,1:T(8,128)}, f32[8,2,8,256]{3,2,0,1:T(8,128)}, u32[]{:S(2)}, u32[]{:S(2)}) collective-permute-start(f32[8,2,8,256]{3,2,0,1:T(8,128)} %get-tuple-element.218), channel_id=1, source_target_pairs={{8,0},{16,8},{24,16},{32,24},{40,32},{48,40},{56,48},{64,56},{72,6... | collective-permute-start | bytes 393224 | tf_op jit(solution)/shard_map/while/body/eval_jaxpr/ppermute | solution.py:27
  87.8 6.8 %collective-permute-start.2 = (f32[8,2,16,256]{3,2,0,1:T(8,128)S(1)}, f32[8,2,16,256]{3,2,0,1:T(8,128)S(1)}, u32[]{:S(2)}, u32[]{:S(2)}) collective-permute-start(f32[8,2,16,256]{3,2,0,1:T(8,128)S(1)} %get-tuple-element.252), channel_id=1, source_target_pairs={{0,1},{1,2},{2,3},{3,4},{4,5},{5,6},{6,7},{8,9},{9,10},{10,11},{11... | collective-permute-start | bytes 786440 | tf_op jit(solution)/shard_map/while/body/eval_jaxpr/ppermute | solution.py:37
  98.5 6.0 %collective-permute-start.1 = (f32[8,2,8,256]{3,2,0,1:T(8,128)}, f32[8,2,8,256]{3,2,0,1:T(8,128)}, u32[]{:S(2)}, u32[]{:S(2)}) collective-permute-start(f32[8,2,8,256]{3,2,0,1:T(8,128)} %get-tuple-element.218), channel_id=1, source_target_pairs={{8,0},{16,8},{24,16},{32,24},{40,32},{48,40},{56,48},{64,56},{72,6... | collective-permute-start | bytes 393224 | tf_op jit(solution)/shard_map/while/body/eval_jaxpr/ppermute | solution.py:27
  119.3 7.5 %collective-permute-start.2 = (f32[8,2,16,256]{3,2,0,1:T(8,128)S(1)}, f32[8,2,16,256]{3,2,0,1:T(8,128)S(1)}, u32[]{:S(2)}, u32[]{:S(2)}) collective-permute-start(f32[8,2,16,256]{3,2,0,1:T(8,128)S(1)} %get-tuple-element.252), channel_id=1, source_target_pairs={{0,1},{1,2},{2,3},{3,4},{4,5},{5,6},{6,7},{8,9},{9,10},{10,11},{11... | collective-permute-start | bytes 786440 | tf_op jit(solution)/shard_map/while/body/eval_jaxpr/ppermute | solution.py:37
  130.7 6.0 %collective-permute-start.1 = (f32[8,2,8,256]{3,2,0,1:T(8,128)}, f32[8,2,8,256]{3,2,0,1:T(8,128)}, u32[]{:S(2)}, u32[]{:S(2)}) collective-permute-start(f32[8,2,8,256]{3,2,0,1:T(8,128)} %get-tuple-element.218), channel_id=1, source_target_pairs={{8,0},{16,8},{24,16},{32,24},{40,32},{48,40},{56,48},{64,56},{72,6... | collective-permute-start | bytes 393224 | tf_op jit(solution)/shard_map/while/body/eval_jaxpr/ppermute | solution.py:27
  151.5 7.6 %collective-permute-start.2 = (f32[8,2,16,256]{3,2,0,1:T(8,128)S(1)}, f32[8,2,16,256]{3,2,0,1:T(8,128)S(1)}, u32[]{:S(2)}, u32[]{:S(2)}) collective-permute-start(f32[8,2,16,256]{3,2,0,1:T(8,128)S(1)} %get-tuple-element.252), channel_id=1, source_target_pairs={{0,1},{1,2},{2,3},{3,4},{4,5},{5,6},{6,7},{8,9},{9,10},{10,11},{11... | collective-permute-start | bytes 786440 | tf_op jit(solution)/shard_map/while/body/eval_jaxpr/ppermute | solution.py:37
  162.9 6.0 %collective-permute-start.1 = (f32[8,2,8,256]{3,2,0,1:T(8,128)}, f32[8,2,8,256]{3,2,0,1:T(8,128)}, u32[]{:S(2)}, u32[]{:S(2)}) collective-permute-start(f32[8,2,8,256]{3,2,0,1:T(8,128)} %get-tuple-element.218), channel_id=1, source_target_pairs={{8,0},{16,8},{24,16},{32,24},{40,32},{48,40},{56,48},{64,56},{72,6... | collective-permute-start | bytes 393224 | tf_op jit(solution)/shard_map/while/body/eval_jaxpr/ppermute | solution.py:27
  183.7 7.6 %collective-permute-start.2 = (f32[8,2,16,256]{3,2,0,1:T(8,128)S(1)}, f32[8,2,16,256]{3,2,0,1:T(8,128)S(1)}, u32[]{:S(2)}, u32[]{:S(2)}) collective-permute-start(f32[8,2,16,256]{3,2,0,1:T(8,128)S(1)} %get-tuple-element.252), channel_id=1, source_target_pairs={{0,1},{1,2},{2,3},{3,4},{4,5},{5,6},{6,7},{8,9},{9,10},{10,11},{11... | collective-permute-start | bytes 786440 | tf_op jit(solution)/shard_map/while/body/eval_jaxpr/ppermute | solution.py:37
  195.1 6.0 %collective-permute-start.1 = (f32[8,2,8,256]{3,2,0,1:T(8,128)}, f32[8,2,8,256]{3,2,0,1:T(8,128)}, u32[]{:S(2)}, u32[]{:S(2)}) collective-permute-start(f32[8,2,8,256]{3,2,0,1:T(8,128)} %get-tuple-element.218), channel_id=1, source_target_pairs={{8,0},{16,8},{24,16},{32,24},{40,32},{48,40},{56,48},{64,56},{72,6... | collective-permute-start | bytes 393224 | tf_op jit(solution)/shard_map/while/body/eval_jaxpr/ppermute | solution.py:27
  215.9 7.6 %collective-permute-start.2 = (f32[8,2,16,256]{3,2,0,1:T(8,128)S(1)}, f32[8,2,16,256]{3,2,0,1:T(8,128)S(1)}, u32[]{:S(2)}, u32[]{:S(2)}) collective-permute-start(f32[8,2,16,256]{3,2,0,1:T(8,128)S(1)} %get-tuple-element.252), channel_id=1, source_target_pairs={{0,1},{1,2},{2,3},{3,4},{4,5},{5,6},{6,7},{8,9},{9,10},{10,11},{11... | collective-permute-start | bytes 786440 | tf_op jit(solution)/shard_map/while/body/eval_jaxpr/ppermute | solution.py:37
  227.3 6.0 %collective-permute-start.1 = (f32[8,2,8,256]{3,2,0,1:T(8,128)}, f32[8,2,8,256]{3,2,0,1:T(8,128)}, u32[]{:S(2)}, u32[]{:S(2)}) collective-permute-start(f32[8,2,8,256]{3,2,0,1:T(8,128)} %get-tuple-element.218), channel_id=1, source_target_pairs={{8,0},{16,8},{24,16},{32,24},{40,32},{48,40},{56,48},{64,56},{72,6... | collective-permute-start | bytes 393224 | tf_op jit(solution)/shard_map/while/body/eval_jaxpr/ppermute | solution.py:27
  248.1 7.6 %collective-permute-start.2 = (f32[8,2,16,256]{3,2,0,1:T(8,128)S(1)}, f32[8,2,16,256]{3,2,0,1:T(8,128)S(1)}, u32[]{:S(2)}, u32[]{:S(2)}) collective-permute-start(f32[8,2,16,256]{3,2,0,1:T(8,128)S(1)} %get-tuple-element.252), channel_id=1, source_target_pairs={{0,1},{1,2},{2,3},{3,4},{4,5},{5,6},{6,7},{8,9},{9,10},{10,11},{11... | collective-permute-start | bytes 786440 | tf_op jit(solution)/shard_map/while/body/eval_jaxpr/ppermute | solution.py:37
  259.5 6.0 %collective-permute-start.1 = (f32[8,2,8,256]{3,2,0,1:T(8,128)}, f32[8,2,8,256]{3,2,0,1:T(8,128)}, u32[]{:S(2)}, u32[]{:S(2)}) collective-permute-start(f32[8,2,8,256]{3,2,0,1:T(8,128)} %get-tuple-element.218), channel_id=1, source_target_pairs={{8,0},{16,8},{24,16},{32,24},{40,32},{48,40},{56,48},{64,56},{72,6... | collective-permute-start | bytes 393224 | tf_op jit(solution)/shard_map/while/body/eval_jaxpr/ppermute | solution.py:27
  280.3 7.8 %collective-permute-start.2 = (f32[8,2,16,256]{3,2,0,1:T(8,128)S(1)}, f32[8,2,16,256]{3,2,0,1:T(8,128)S(1)}, u32[]{:S(2)}, u32[]{:S(2)}) collective-permute-start(f32[8,2,16,256]{3,2,0,1:T(8,128)S(1)} %get-tuple-element.252), channel_id=1, source_target_pairs={{0,1},{1,2},{2,3},{3,4},{4,5},{5,6},{6,7},{8,9},{9,10},{10,11},{11... | collective-permute-start | bytes 786440 | tf_op jit(solution)/shard_map/while/body/eval_jaxpr/ppermute | solution.py:37
  292.1 13.8 %copy.27 = f32[5,8,16,256]{0,2,1,3:T(8,128)} copy(f32[5,8,16,256]{3,0,2,1:T(8,128)S(1)} %fusion.33) | data formatting | bytes 1310720
  305.9 11.9 %reshape.106 = f32[256,640]{1,0:T(8,128)} reshape(f32[256,8,16,5]{3,2,1,0:T(8,128)} %bitcast.211) | data formatting | bytes 1310720
  318.6 43.0 %reduce-scatter.4.cloned.1.call-done = f32[64,640]{1,0:T(8,128)} async-done(((f32[256,640]{1,0:T(8,128)}), f32[64,640]{1,0:T(8,128)}) %reduce-scatter.4.cloned.1.call-update) | async-done | bytes 163856
  361.5 6.2 %reshape.107 = f32[64,8,16,5]{3,2,1,0:T(8,128)} reshape(f32[64,640]{1,0:T(8,128)} %reduce-scatter.4.cloned.1.call-done) | data formatting | bytes 327680
  373.9 45.2 %all_gather.3 = f32[5,8,16,256]{2,1,0,3:T(8,128)S(1)} all-gather(f32[5,8,16,64]{2,1,0,3:T(8,128)S(1)} %copy.14), channel_id=1, replica_groups=mesh['band'=4,'tile'=16,'slab'=8] {'band'}, dimensions={3}, use_global_device_ids=true | all-gather | bytes 819200 | tf_op jit(solution)/shard_map/all_gather | solution.py:126
  (654 shorter events, 174.3 us)
Async XLA Ops:
  7.2 354.4 %reduce-scatter.4.cloned.1.call-start = ((), (), s32[]{:S(2)}) async-start(), calls=%async_computation.1 | async-start | bytes 819200
  8.7 21.3 %collective-permute-start.3 = (f32[7,8,8,256]{3,2,1,0:T(8,128)S(1)}, f32[7,8,8,256]{3,2,1,0:T(8,128)S(1)}, u32[]{:S(2)}, u32[]{:S(2)}) collective-permute-start(f32[7,8,8,256]{3,2,1,0:T(8,128)S(1)} %get-tuple-element.112), channel_id=1, source_target_pairs={{0,8},{8,16},{16,24},{24,32},{32,40},{40,48},{48,56},{56,64},{64,7... | collective-permute-start | bytes 1376264 | tf_op jit(solution)/shard_map/ppermute | solution.py:25
  13.0 18.2 %collective-permute-start.4 = (f32[7,8,8,256]{3,2,1,0:T(8,128)S(1)}, f32[7,8,8,256]{3,2,1,0:T(8,128)}, u32[]{:S(2)}, u32[]{:S(2)}) collective-permute-start(f32[7,8,8,256]{3,2,1,0:T(8,128)S(1)} %get-tuple-element.113), channel_id=1, source_target_pairs={{8,0},{16,8},{24,16},{32,24},{40,32},{48,40},{56,48},{64,56},{72,6... | collective-permute-start | bytes 1376264 | tf_op jit(solution)/shard_map/ppermute | solution.py:27
  38.6 13.2 %collective-permute-start = (f32[8,2,8,256]{3,2,0,1:T(8,128)}, f32[8,2,8,256]{3,2,0,1:T(8,128)}, u32[]{:S(2)}, u32[]{:S(2)}) collective-permute-start(f32[8,2,8,256]{3,2,0,1:T(8,128)} %get-tuple-element.217), channel_id=1, source_target_pairs={{0,8},{8,16},{16,24},{24,32},{32,40},{40,48},{48,56},{56,64},{64,7... | collective-permute-start | bytes 393224 | tf_op jit(solution)/shard_map/while/body/eval_jaxpr/ppermute | solution.py:25
  40.5 13.1 %collective-permute-start.1 = (f32[8,2,8,256]{3,2,0,1:T(8,128)}, f32[8,2,8,256]{3,2,0,1:T(8,128)}, u32[]{:S(2)}, u32[]{:S(2)}) collective-permute-start(f32[8,2,8,256]{3,2,0,1:T(8,128)} %get-tuple-element.218), channel_id=1, source_target_pairs={{8,0},{16,8},{24,16},{32,24},{40,32},{48,40},{56,48},{64,56},{72,6... | collective-permute-start | bytes 393224 | tf_op jit(solution)/shard_map/while/body/eval_jaxpr/ppermute | solution.py:27
  65.1 12.6 %collective-permute-start = (f32[8,2,8,256]{3,2,0,1:T(8,128)}, f32[8,2,8,256]{3,2,0,1:T(8,128)}, u32[]{:S(2)}, u32[]{:S(2)}) collective-permute-start(f32[8,2,8,256]{3,2,0,1:T(8,128)} %get-tuple-element.217), channel_id=1, source_target_pairs={{0,8},{8,16},{16,24},{24,32},{32,40},{40,48},{48,56},{56,64},{64,7... | collective-permute-start | bytes 393224 | tf_op jit(solution)/shard_map/while/body/eval_jaxpr/ppermute | solution.py:25
  67.0 12.6 %collective-permute-start.1 = (f32[8,2,8,256]{3,2,0,1:T(8,128)}, f32[8,2,8,256]{3,2,0,1:T(8,128)}, u32[]{:S(2)}, u32[]{:S(2)}) collective-permute-start(f32[8,2,8,256]{3,2,0,1:T(8,128)} %get-tuple-element.218), channel_id=1, source_target_pairs={{8,0},{16,8},{24,16},{32,24},{40,32},{48,40},{56,48},{64,56},{72,6... | collective-permute-start | bytes 393224 | tf_op jit(solution)/shard_map/while/body/eval_jaxpr/ppermute | solution.py:27
  96.6 12.6 %collective-permute-start = (f32[8,2,8,256]{3,2,0,1:T(8,128)}, f32[8,2,8,256]{3,2,0,1:T(8,128)}, u32[]{:S(2)}, u32[]{:S(2)}) collective-permute-start(f32[8,2,8,256]{3,2,0,1:T(8,128)} %get-tuple-element.217), channel_id=1, source_target_pairs={{0,8},{8,16},{16,24},{24,32},{32,40},{40,48},{48,56},{56,64},{64,7... | collective-permute-start | bytes 393224 | tf_op jit(solution)/shard_map/while/body/eval_jaxpr/ppermute | solution.py:25
  98.5 12.6 %collective-permute-start.1 = (f32[8,2,8,256]{3,2,0,1:T(8,128)}, f32[8,2,8,256]{3,2,0,1:T(8,128)}, u32[]{:S(2)}, u32[]{:S(2)}) collective-permute-start(f32[8,2,8,256]{3,2,0,1:T(8,128)} %get-tuple-element.218), channel_id=1, source_target_pairs={{8,0},{16,8},{24,16},{32,24},{40,32},{48,40},{56,48},{64,56},{72,6... | collective-permute-start | bytes 393224 | tf_op jit(solution)/shard_map/while/body/eval_jaxpr/ppermute | solution.py:27
  128.7 12.6 %collective-permute-start = (f32[8,2,8,256]{3,2,0,1:T(8,128)}, f32[8,2,8,256]{3,2,0,1:T(8,128)}, u32[]{:S(2)}, u32[]{:S(2)}) collective-permute-start(f32[8,2,8,256]{3,2,0,1:T(8,128)} %get-tuple-element.217), channel_id=1, source_target_pairs={{0,8},{8,16},{16,24},{24,32},{32,40},{40,48},{48,56},{56,64},{64,7... | collective-permute-start | bytes 393224 | tf_op jit(solution)/shard_map/while/body/eval_jaxpr/ppermute | solution.py:25
  130.7 12.6 %collective-permute-start.1 = (f32[8,2,8,256]{3,2,0,1:T(8,128)}, f32[8,2,8,256]{3,2,0,1:T(8,128)}, u32[]{:S(2)}, u32[]{:S(2)}) collective-permute-start(f32[8,2,8,256]{3,2,0,1:T(8,128)} %get-tuple-element.218), channel_id=1, source_target_pairs={{8,0},{16,8},{24,16},{32,24},{40,32},{48,40},{56,48},{64,56},{72,6... | collective-permute-start | bytes 393224 | tf_op jit(solution)/shard_map/while/body/eval_jaxpr/ppermute | solution.py:27
  151.5 8.7 %collective-permute-start.2 = (f32[8,2,16,256]{3,2,0,1:T(8,128)S(1)}, f32[8,2,16,256]{3,2,0,1:T(8,128)S(1)}, u32[]{:S(2)}, u32[]{:S(2)}) collective-permute-start(f32[8,2,16,256]{3,2,0,1:T(8,128)S(1)} %get-tuple-element.252), channel_id=1, source_target_pairs={{0,1},{1,2},{2,3},{3,4},{4,5},{5,6},{6,7},{8,9},{9,10},{10,11},{11... | collective-permute-start | bytes 786440 | tf_op jit(solution)/shard_map/while/body/eval_jaxpr/ppermute | solution.py:37
  160.9 12.6 %collective-permute-start = (f32[8,2,8,256]{3,2,0,1:T(8,128)}, f32[8,2,8,256]{3,2,0,1:T(8,128)}, u32[]{:S(2)}, u32[]{:S(2)}) collective-permute-start(f32[8,2,8,256]{3,2,0,1:T(8,128)} %get-tuple-element.217), channel_id=1, source_target_pairs={{0,8},{8,16},{16,24},{24,32},{32,40},{40,48},{48,56},{56,64},{64,7... | collective-permute-start | bytes 393224 | tf_op jit(solution)/shard_map/while/body/eval_jaxpr/ppermute | solution.py:25
  162.9 12.6 %collective-permute-start.1 = (f32[8,2,8,256]{3,2,0,1:T(8,128)}, f32[8,2,8,256]{3,2,0,1:T(8,128)}, u32[]{:S(2)}, u32[]{:S(2)}) collective-permute-start(f32[8,2,8,256]{3,2,0,1:T(8,128)} %get-tuple-element.218), channel_id=1, source_target_pairs={{8,0},{16,8},{24,16},{32,24},{40,32},{48,40},{56,48},{64,56},{72,6... | collective-permute-start | bytes 393224 | tf_op jit(solution)/shard_map/while/body/eval_jaxpr/ppermute | solution.py:27
  183.7 8.7 %collective-permute-start.2 = (f32[8,2,16,256]{3,2,0,1:T(8,128)S(1)}, f32[8,2,16,256]{3,2,0,1:T(8,128)S(1)}, u32[]{:S(2)}, u32[]{:S(2)}) collective-permute-start(f32[8,2,16,256]{3,2,0,1:T(8,128)S(1)} %get-tuple-element.252), channel_id=1, source_target_pairs={{0,1},{1,2},{2,3},{3,4},{4,5},{5,6},{6,7},{8,9},{9,10},{10,11},{11... | collective-permute-start | bytes 786440 | tf_op jit(solution)/shard_map/while/body/eval_jaxpr/ppermute | solution.py:37
  193.2 12.6 %collective-permute-start = (f32[8,2,8,256]{3,2,0,1:T(8,128)}, f32[8,2,8,256]{3,2,0,1:T(8,128)}, u32[]{:S(2)}, u32[]{:S(2)}) collective-permute-start(f32[8,2,8,256]{3,2,0,1:T(8,128)} %get-tuple-element.217), channel_id=1, source_target_pairs={{0,8},{8,16},{16,24},{24,32},{32,40},{40,48},{48,56},{56,64},{64,7... | collective-permute-start | bytes 393224 | tf_op jit(solution)/shard_map/while/body/eval_jaxpr/ppermute | solution.py:25
  195.1 12.6 %collective-permute-start.1 = (f32[8,2,8,256]{3,2,0,1:T(8,128)}, f32[8,2,8,256]{3,2,0,1:T(8,128)}, u32[]{:S(2)}, u32[]{:S(2)}) collective-permute-start(f32[8,2,8,256]{3,2,0,1:T(8,128)} %get-tuple-element.218), channel_id=1, source_target_pairs={{8,0},{16,8},{24,16},{32,24},{40,32},{48,40},{56,48},{64,56},{72,6... | collective-permute-start | bytes 393224 | tf_op jit(solution)/shard_map/while/body/eval_jaxpr/ppermute | solution.py:27
  215.9 8.7 %collective-permute-start.2 = (f32[8,2,16,256]{3,2,0,1:T(8,128)S(1)}, f32[8,2,16,256]{3,2,0,1:T(8,128)S(1)}, u32[]{:S(2)}, u32[]{:S(2)}) collective-permute-start(f32[8,2,16,256]{3,2,0,1:T(8,128)S(1)} %get-tuple-element.252), channel_id=1, source_target_pairs={{0,1},{1,2},{2,3},{3,4},{4,5},{5,6},{6,7},{8,9},{9,10},{10,11},{11... | collective-permute-start | bytes 786440 | tf_op jit(solution)/shard_map/while/body/eval_jaxpr/ppermute | solution.py:37
  225.4 12.6 %collective-permute-start = (f32[8,2,8,256]{3,2,0,1:T(8,128)}, f32[8,2,8,256]{3,2,0,1:T(8,128)}, u32[]{:S(2)}, u32[]{:S(2)}) collective-permute-start(f32[8,2,8,256]{3,2,0,1:T(8,128)} %get-tuple-element.217), channel_id=1, source_target_pairs={{0,8},{8,16},{16,24},{24,32},{32,40},{40,48},{48,56},{56,64},{64,7... | collective-permute-start | bytes 393224 | tf_op jit(solution)/shard_map/while/body/eval_jaxpr/ppermute | solution.py:25
  227.3 12.6 %collective-permute-start.1 = (f32[8,2,8,256]{3,2,0,1:T(8,128)}, f32[8,2,8,256]{3,2,0,1:T(8,128)}, u32[]{:S(2)}, u32[]{:S(2)}) collective-permute-start(f32[8,2,8,256]{3,2,0,1:T(8,128)} %get-tuple-element.218), channel_id=1, source_target_pairs={{8,0},{16,8},{24,16},{32,24},{40,32},{48,40},{56,48},{64,56},{72,6... | collective-permute-start | bytes 393224 | tf_op jit(solution)/shard_map/while/body/eval_jaxpr/ppermute | solution.py:27
  248.1 8.7 %collective-permute-start.2 = (f32[8,2,16,256]{3,2,0,1:T(8,128)S(1)}, f32[8,2,16,256]{3,2,0,1:T(8,128)S(1)}, u32[]{:S(2)}, u32[]{:S(2)}) collective-permute-start(f32[8,2,16,256]{3,2,0,1:T(8,128)S(1)} %get-tuple-element.252), channel_id=1, source_target_pairs={{0,1},{1,2},{2,3},{3,4},{4,5},{5,6},{6,7},{8,9},{9,10},{10,11},{11... | collective-permute-start | bytes 786440 | tf_op jit(solution)/shard_map/while/body/eval_jaxpr/ppermute | solution.py:37
  257.6 12.6 %collective-permute-start = (f32[8,2,8,256]{3,2,0,1:T(8,128)}, f32[8,2,8,256]{3,2,0,1:T(8,128)}, u32[]{:S(2)}, u32[]{:S(2)}) collective-permute-start(f32[8,2,8,256]{3,2,0,1:T(8,128)} %get-tuple-element.217), channel_id=1, source_target_pairs={{0,8},{8,16},{16,24},{24,32},{32,40},{40,48},{48,56},{56,64},{64,7... | collective-permute-start | bytes 393224 | tf_op jit(solution)/shard_map/while/body/eval_jaxpr/ppermute | solution.py:25
  259.5 12.6 %collective-permute-start.1 = (f32[8,2,8,256]{3,2,0,1:T(8,128)}, f32[8,2,8,256]{3,2,0,1:T(8,128)}, u32[]{:S(2)}, u32[]{:S(2)}) collective-permute-start(f32[8,2,8,256]{3,2,0,1:T(8,128)} %get-tuple-element.218), channel_id=1, source_target_pairs={{8,0},{16,8},{24,16},{32,24},{40,32},{48,40},{56,48},{64,56},{72,6... | collective-permute-start | bytes 393224 | tf_op jit(solution)/shard_map/while/body/eval_jaxpr/ppermute | solution.py:27
  280.3 9.0 %collective-permute-start.2 = (f32[8,2,16,256]{3,2,0,1:T(8,128)S(1)}, f32[8,2,16,256]{3,2,0,1:T(8,128)S(1)}, u32[]{:S(2)}, u32[]{:S(2)}) collective-permute-start(f32[8,2,16,256]{3,2,0,1:T(8,128)S(1)} %get-tuple-element.252), channel_id=1, source_target_pairs={{0,1},{1,2},{2,3},{3,4},{4,5},{5,6},{6,7},{8,9},{9,10},{10,11},{11... | collective-permute-start | bytes 786440 | tf_op jit(solution)/shard_map/while/body/eval_jaxpr/ppermute | solution.py:37
  (76 other events, 603.8 us)
Sparse Core Ops, SparseCore 0:
  317.9 43.5 reduce-scatter.3
where the time goes:
time: 438 us; the launch traced here: 435 us
  starting transfers between devices  131 us (30%)
  local copies, waits for them, and re-layouts  107 us (24%)
  other arithmetic  69.3 us (16%)
  waiting for transfers between devices  59.8 us (14%)
  blocking collectives  45.2 us (10%)
  between operations  14.3 us (3%)
  matrix products  5.26 us (1%)
    ppermute x9, starting transfers between devices, extended_2(): lax.ppermute(head, axis, [((i + 1) % count, i) for i in range(ends)])  57.3 us
    ppermute x8, starting transfers between devices, shifted(): return lax.ppermute(block, axis, route)  53.7 us
    add x64, other arithmetic, sweep(): attenuation * ((1.0 - TILT_SHARE) * intensity + TILT_SHARE * upwind)  51.4 us
    all_gather x1, blocking collectives, per_device(): lax.all_gather(populations_share, 'band', axis=3, tiled=True)  45.2 us
    unnamed x29, local copies, waits for them, and re-layouts  43.1 us
    unnamed x2, waiting for transfers between devices  43 us
    while x200, local copies, waits for them, and re-layouts  35.4 us
    ppermute x9, starting transfers between devices, extended_2(): lax.ppermute(tail, axis, [(i, (i + 1) % count) for i in range(ends)])  19.6 us
  transfers between devices with their start and end apart: 27, of which 11 were waited for; matrix products, arithmetic and copies ran while one was open for 12% of the time, Pallas kernels for 0%

commit v1 on v0

v1 whole, which is shorter than its diff:
```python
import jax
import jax.numpy as jnp
from jax import lax
from jax.experimental import pallas as pl
from jax.experimental.pallas import tpu as pltpu
from jax.sharding import PartitionSpec as P

LINES = 5
EPS_THERMAL = 0.1
COLLISION = 0.5
PATH_FACTOR = 1.25
TILT_SHARE = 0.4
LOG2E = 1.4426950408889634
LANES = 128
FIELDS = 6
PLANE = ("slab", "tile")


def line_ratios(l1, l2, l3, l4):
    return (
        l3 / (1.0 + l3),
        l4 / (1.0 + l4),
        l3 / (l1 + l3),
        l4 / (l1 + l4),
        l4 / (l2 + l4),
    )


def pack_kernel(band_ref, opacity_ref, planck_ref, levels_ref, out_ref, turned_ref):
    half = pl.multiple_of((band_ref[0] % 2) * 64, 64)
    inverse = 1.0 / levels_ref[0]
    fields = [opacity_ref[...], planck_ref[...]]
    fields += [levels_ref[k] * inverse for k in range(1, 5)]
    for i, field in enumerate(fields):
        turned_ref[i] = field.T
        rows = turned_ref[i, pl.ds(half, 64), :]
        out_ref[pl.ds(i, 64, stride=2 * FIELDS), :] = rows
        out_ref[pl.ds(FIELDS + i, 64, stride=2 * FIELDS), :] = rows


def sweep_kernel(half_ref, in_ref, *refs):
    *param_refs, out_ref, w_ref, v_ref, y_ref, j_ref = refs
    params = param_refs[0][...]
    for ref in param_refs[1:]:
        params = params + ref[...]
    decay = params[0:1] * (-PATH_FACTOR * LOG2E)
    weight = params[1:2]
    line = params[2:3].astype(jnp.int32)
    lane = lax.broadcasted_iota(jnp.int32, (1, LANES), 1)
    lane_tile = (lane // 32) * 4
    row = lax.broadcasted_iota(jnp.int32, (96, LANES), 0)
    row_field, row_tile = row // 16, row % 16
    for c in range(4):
        same = row_tile == lane_tile + c
        for k, want in enumerate((jnp.zeros_like(line), line + 1)):
            hit = jnp.where(same & (row_field == want), 1.0, 0.0).astype(jnp.bfloat16)
            at = c * 256 + k * LANES
            w_ref[0:96, at : at + LANES] = hit
            w_ref[96:192, at : at + LANES] = hit
    row = lax.broadcasted_iota(jnp.int32, (80, LANES), 0)
    row_line, row_tile = row // 16, row % 16
    for c in range(4):
        hit = jnp.where((row_tile == lane_tile + c) & (row_line == line), 1.0, 0.0)
        hit = hit.astype(jnp.bfloat16)
        v_ref[:, c * LANES : (c + 1) * LANES] = hit
        v_ref[:, 512 + c * LANES : 512 + (c + 1) * LANES] = hit

    sub = lax.broadcasted_iota(jnp.int32, (8, LANES), 0)
    first_row, last_row = sub == 0, sub == 7
    lane8 = lax.broadcasted_iota(jnp.int32, (8, LANES), 1)
    inner_left, inner_right = lane8 >= 32, lane8 < 96
    half = half_ref[0]

    def slab(s, state):
        base = s * 96
        op, pk, r1, r2, r3, r4 = [in_ref[pl.ds(base + i, 16, stride=FIELDS), :] for i in range(6)]
        sources = [EPS_THERMAL * pk + (1.0 - EPS_THERMAL) * q for q in line_ratios(r1, r2, r3, r4)]
        parts = jnp.concatenate([op, *sources], axis=0)
        high = parts.astype(jnp.bfloat16)
        low = (parts - high.astype(jnp.float32)).astype(jnp.bfloat16)
        y_ref[...] = lax.dot_general(
            jnp.concatenate([high, low], axis=0),
            w_ref[...],
            (((0,), (0,)), ((), ())),
            preferred_element_type=jnp.float32,
        )
        right, left = list(state[:8]), list(state[8:])
        for z in range(8):
            turned = [pltpu.roll(v, 1, 0) for v in right]
            edge = jnp.where(inner_left, pltpu.roll(turned[7], 32, 1), 0.0)
            up_right = [jnp.where(first_row, turned[p - 1] if p else edge, turned[p]) for p in range(8)]
            turned = [pltpu.roll(v, 7, 0) for v in left]
            edge = jnp.where(inner_right, pltpu.roll(turned[0], 96, 1), 0.0)
            up_left = [jnp.where(last_row, turned[p + 1] if p < 7 else edge, turned[p]) for p in range(8)]
            for c in range(4):
                sums = []
                for k in range(2):
                    p = 2 * c + k
                    rows = slice(z * 16 + k * 8, z * 16 + k * 8 + 8)
                    a = jnp.exp2(y_ref[rows, c * 256 : c * 256 + 128] * decay)
                    b = (1.0 - a) * y_ref[rows, c * 256 + 128 : c * 256 + 256]
                    right[p] = a * ((1.0 - TILT_SHARE) * right[p] + TILT_SHARE * up_right[p]) + b
                    left[p] = a * ((1.0 - TILT_SHARE) * left[p] + TILT_SHARE * up_left[p]) + b
                    sums.append((right[p] + left[p]) * weight)
                both = jnp.concatenate(sums, axis=0)
                high = both.astype(jnp.bfloat16)
                low = (both - high.astype(jnp.float32)).astype(jnp.bfloat16)
                j_ref[z * 16 : z * 16 + 16, c * LANES : (c + 1) * LANES] = high
                j_ref[z * 16 : z * 16 + 16, 512 + c * LANES : 512 + (c + 1) * LANES] = low
        jbar = lax.dot_general(
            v_ref[...], j_ref[...], (((1,), (1,)), ((), ())), preferred_element_type=jnp.float32
        )
        jbar = [jbar[16 * t : 16 * t + 16] for t in range(LINES)]
        ratio = [(j + COLLISION * pk) / (1.0 + j + COLLISION) for j in jbar]
        level_1 = 0.5 * (ratio[0] / ratio[2] + ratio[1] / ratio[3])
        level_2 = ratio[1] / ratio[4]
        out_ref[pl.ds(s * 32, 16, stride=2), :] = jnp.where(half == 0, level_1, ratio[0])
        out_ref[pl.ds(s * 32 + 1, 16, stride=2), :] = jnp.where(half == 0, level_2, ratio[1])
        return tuple(right) + tuple(left)

    lax.fori_loop(0, 8, slab, (jnp.zeros((8, LANES), jnp.float32),) * 16)


def finish_kernel(band_ref, line_ref, in_ref, planck_ref, levels_ref, source_ref, lines_ref):
    l1, l2, l3, l4 = [in_ref[pl.ds(k, 256, stride=4), :].T for k in range(4)]
    for t, q in enumerate(line_ratios(l1, l2, l3, l4)):
        lines_ref[t] = (1.0 - EPS_THERMAL) * q
    thermal = EPS_THERMAL * planck_ref[...]
    for f in range(8):
        source_ref[f] = thermal + lines_ref[line_ref[f]]
    start = band_ref[0] * 256
    own = [in_ref[pl.ds(start + k, 64, stride=4), :] for k in range(4)]
    share = 1.0 / (1.0 + own[0] + own[1] + own[2] + own[3])
    levels_ref[0] = share.T
    for k in range(4):
        levels_ref[k + 1] = (own[k] * share).T


def per_device(strength, opacity, planck, old_populations, line_index, line_weight):
    band = lax.axis_index("band")
    vmem = pl.BlockSpec(memory_space=pltpu.VMEM)
    smem = pl.BlockSpec(memory_space=pltpu.SMEM)
    band_1 = band.astype(jnp.int32).reshape(1)
    half_1 = (lax.axis_index("tile") % 2).astype(jnp.int32).reshape(1)

    own = jnp.stack([strength, line_weight * (LINES / 64.0), line_index.astype(jnp.float32)])
    own = jnp.broadcast_to(own[:, None, None, :], (3, 4, 4, 8))
    mine = (jnp.arange(4) == band)[None, None, :, None]
    own = jnp.where(mine, own, 0.0).reshape(3, LANES)
    own = jnp.concatenate([own, jnp.zeros((5, LANES), jnp.float32)], axis=0)
    params = [own] + [
        lax.ppermute(own, "band", [(i, (i + d) % 4) for i in range(4)]) for d in (1, 2, 3)
    ]

    planck_2d = planck.reshape(128, 256)
    packed = pl.pallas_call(
        pack_kernel,
        grid_spec=pltpu.PrefetchScalarGridSpec(
            num_scalar_prefetch=1,
            grid=(1,),
            in_specs=[
                pl.BlockSpec((128, 128), lambda i, b: (0, b[0] // 2)),
                pl.BlockSpec((128, 128), lambda i, b: (0, b[0] // 2)),
                pl.BlockSpec((5, 128, 128), lambda i, b: (0, 0, b[0] // 2)),
            ],
            out_specs=pl.BlockSpec((128 * FIELDS, LANES), lambda i, b: (0, 0)),
            scratch_shapes=[pltpu.VMEM((FIELDS, 128, 128), jnp.float32)],
        ),
        out_shape=jax.ShapeDtypeStruct((128 * FIELDS, LANES), jnp.float32),
        name="pack",
    )(band_1, opacity.reshape(128, 256), planck_2d, old_populations.reshape(5, 128, 256))

    plane = lax.all_to_all(packed.reshape(128, 3, 2, LANES), PLANE, 0, 0, tiled=True)

    swept = pl.pallas_call(
        sweep_kernel,
        in_specs=[smem, vmem] + [vmem] * len(params),
        out_specs=vmem,
        out_shape=jax.ShapeDtypeStruct((256, LANES), jnp.float32),
        scratch_shapes=[
            pltpu.VMEM((192, 1024), jnp.bfloat16),
            pltpu.VMEM((80, 1024), jnp.bfloat16),
            pltpu.VMEM((128, 1024), jnp.float32),
            pltpu.VMEM((128, 1024), jnp.bfloat16),
        ],
        name="sweep",
    )(half_1, plane.reshape(128 * FIELDS, LANES), *params)

    quarter = lax.all_to_all(swept.reshape(128, 2, LANES), PLANE, 0, 0, tiled=True)
    levels = lax.all_gather(quarter.reshape(256, LANES), "band", axis=0, tiled=True)

    new_levels, new_source = pl.pallas_call(
        finish_kernel,
        in_specs=[smem, smem, vmem, vmem],
        out_specs=[vmem, vmem],
        out_shape=[
            jax.ShapeDtypeStruct((5, 128, 64), jnp.float32),
            jax.ShapeDtypeStruct((8, 128, 256), jnp.float32),
        ],
        scratch_shapes=[pltpu.VMEM((LINES, 128, 256), jnp.float32)],
        name="finish",
    )(band_1, line_index, levels, planck_2d)
    return new_levels.reshape(5, 8, 16, 64), new_source.reshape(8, 8, 16, 256)


def solution(mesh):
    in_specs = (
        P("band"),
        P("slab", "tile", None),
        P("slab", "tile", None),
        P(None, "slab", "tile", None),
        P("band"),
        P("band"),
    )
    out_specs = (P(None, "slab", "tile", "band"), P("band", "slab", "tile", None))
    return jax.shard_map(
        per_device, mesh=mesh, in_specs=in_specs, out_specs=out_specs, check_vma=False
    )
```

time: 438 us -> 87 us (0.20)
  local copies, waits for them, and re-layouts: 107 us -> 2.89 us
  starting transfers between devices: 131 us -> 27.5 us
  other arithmetic: 69.3 us -> 0.03 us
  waiting for transfers between devices: 59.8 us -> 4.98 us
  between operations: 14.3 us -> 0.76 us
  Pallas kernels: 0 us -> 11.8 us
  blocking collectives: 45.2 us -> 38.6 us
  matrix products: 5.26 us -> 0 us
    ppermute x26 -> x3, starting transfers between devices: 131 us -> 10.2 us  [per_device(): lax.ppermute(own, 'band', [(i, (i + d) % 4) for i in range(4)])]
    add x65 -> x0, other arithmetic: 51.5 us -> none  [the longest x64 51.4 us: sweep(): attenuation * ((1.0 - TILT_SHARE) * intensity + TILT_SHARE * upwind)]
    unnamed x2 -> x0, waiting for transfers between devices: 43 us -> none
    unnamed x29 -> x16, local copies, waits for them, and re-layouts: 43.1 us -> 2.62 us
    while x200 -> x0, local copies, waits for them, and re-layouts: 35.4 us -> none
    all_gather x1, blocking collectives: 45.2 us -> 14.2 us  [per_device(): lax.all_gather(quarter.reshape(256, LANES), 'band', axis=0, tiled=True)]
    all_to_all x0 -> x1, blocking collectives: none -> 24.4 us  [per_device(): lax.all_to_all(swept.reshape(128, 2, LANES), PLANE, 0, 0, tiled=True)]
    all_to_all x0 -> x1, starting transfers between devices: none -> 17.4 us  [per_device(): lax.all_to_all(packed.reshape(128, 3, 2, LANES), PLANE, 0, 0, tiled=True)]
  transfers between devices with their start and end apart: 27 -> 4, of which waited for: 11 -> 3; matrix products, arithmetic and copies ran while one was open for 12% -> 0% of each run, Pallas kernels for 0% -> 0%
where the time goes in v1:
time: 87 us; the launch traced here: 86.6 us
  blocking collectives  38.6 us (44%)
  starting transfers between devices  27.5 us (32%)
  Pallas kernels  11.8 us (14%)
  waiting for transfers between devices  4.98 us (6%)
  local copies, waits for them, and re-layouts  2.89 us (3%)
    all_to_all x1, blocking collectives, per_device(): lax.all_to_all(swept.reshape(128, 2, LANES), PLANE, 0, 0, tiled=True)  24.4 us
    all_to_all x1, starting transfers between devices, per_device(): lax.all_to_all(packed.reshape(128, 3, 2, LANES), PLANE, 0, 0, tiled=True)  17.4 us
    all_gather x1, blocking collectives, per_device(): lax.all_gather(quarter.reshape(256, LANES), 'band', axis=0, tiled=True)  14.2 us
    ppermute x3, starting transfers between devices, per_device(): lax.ppermute(own, 'band', [(i, (i + d) % 4) for i in range(4)])  10.2 us
    pallas_call x1, Pallas kernels, per_device(): pl.pallas_call(sweep_kernel, in_specs=[smem, vmem] + [vmem] * len(params)...  7.37 us
    ppermute x3, waiting for transfers between devices, per_device(): lax.ppermute(own, 'band', [(i, (i + d) % 4) for i in range(4)])  3.88 us
    unnamed x16, local copies, waits for them, and re-layouts  2.62 us
    pallas_call x1, Pallas kernels, per_device(): pl.pallas_call(finish_kernel, in_specs=[smem, smem, vmem, vmem], out_spec...  2.46 us
  transfers between devices with their start and end apart: 4, of which 3 were waited for; matrix products, arithmetic and copies ran while one was open for 0% of the time, Pallas kernels for 0%

profile of v1, /device:TPU:8, one launch (start us, length us, event | category | flops | bytes accessed | tf_op | source)
XLA Modules:
  0.0 86.6 jit_solution(5563305554965555193)
XLA Ops:
  0.6 2.0 %pack.1 = f32[768,128]{1,0:T(8,128)} custom-call(s32[1]{0:T(128)} %bitcast.band_ref, f32[128,256]{1,0:T(8,128)} %bitcast.23, f32[128,256]{1,0:T(8,128)} %bitcast.19, f32[5,128,256]{2,1,0:T(8,128)} %bitcast.18), custom_call_target="tpu_custom_call" | custom-call | tf_op jit(solution)/shard_map/pack/pallas_call | solution.py:156
  2.7 17.4 %all-to-all-start = ((f32[128,3,2,128]{3,2,1,0:T(2,128)}), f32[128,3,2,128]{3,2,1,0:T(2,128)S(1)}, u32[]{:S(2)}, u32[]{:S(2)}) async-start(f32[128,3,2,128]{3,2,1,0:T(2,128)} %bitcast.17), calls=%async_computation | async-start | bytes 786432 | tf_op jit(solution)/shard_map/all_to_all | solution.py:173
  20.0 0.1 broadcast_in_dim.26
  20.1 0.1 broadcast_in_dim.27
  20.2 0.6 copy-done.7
  20.8 0.7 copy-done.5
  21.4 0.7 copy-done.6
  22.1 0.1 broadcast_in_dim.30
  22.2 0.0 copy-start.1
  22.2 4.7 %collective-permute-start.2 = (f32[8,128]{1,0:T(8,128)S(1)}, f32[8,128]{1,0:T(8,128)S(1)}, u32[]{:S(2)}, u32[]{:S(2)}) collective-permute-start(f32[8,128]{1,0:T(8,128)S(1)} %concatenate.3.refs_0_), channel_id=1, source_target_pairs={{0,384},{128,0},{256,128},{384,256},{1,385},{129,1},{257,129},{385... | collective-permute-start | bytes 12296 | tf_op jit(solution)/shard_map/ppermute | solution.py:152
  26.9 2.7 %collective-permute-start.1 = (f32[8,128]{1,0:T(8,128)S(1)}, f32[8,128]{1,0:T(8,128)S(1)}, u32[]{:S(2)}, u32[]{:S(2)}) collective-permute-start(f32[8,128]{1,0:T(8,128)S(1)} %concatenate.3.refs_0_), channel_id=1, source_target_pairs={{0,256},{128,384},{256,0},{384,128},{1,257},{129,385},{257,1},{385... | collective-permute-start | bytes 12296 | tf_op jit(solution)/shard_map/ppermute | solution.py:152
  29.6 2.8 %collective-permute-start = (f32[8,128]{1,0:T(8,128)S(1)}, f32[8,128]{1,0:T(8,128)S(1)}, u32[]{:S(2)}, u32[]{:S(2)}) collective-permute-start(f32[8,128]{1,0:T(8,128)S(1)} %concatenate.3.refs_0_), channel_id=1, source_target_pairs={{0,128},{128,256},{256,384},{384,0},{1,129},{129,257},{257,385},{3... | collective-permute-start | bytes 12296 | tf_op jit(solution)/shard_map/ppermute | solution.py:152
  32.4 0.0 copy-done.1
  32.5 0.0 collective-permute-done.2.refs_3_
  32.5 0.0 copy-start.2
  32.5 1.5 %collective-permute-done.1.refs_2_ = f32[8,128]{1,0:T(8,128)S(1)} collective-permute-done((f32[8,128]{1,0:T(8,128)S(1)}, f32[8,128]{1,0:T(8,128)S(1)}, u32[]{:S(2)}, u32[]{:S(2)}) %collective-permute-start.1) | collective-permute-done | bytes 4128 | tf_op jit(solution)/shard_map/ppermute | solution.py:152
  33.9 2.4 %collective-permute-done.refs_1_ = f32[8,128]{1,0:T(8,128)S(1)} collective-permute-done((f32[8,128]{1,0:T(8,128)S(1)}, f32[8,128]{1,0:T(8,128)S(1)}, u32[]{:S(2)}, u32[]{:S(2)}) %collective-permute-start) | collective-permute-done | bytes 4128 | tf_op jit(solution)/shard_map/ppermute | solution.py:152
  36.4 1.1 %all-to-all-done = f32[128,3,2,128]{3,2,1,0:T(2,128)S(1)} async-done(((f32[128,3,2,128]{3,2,1,0:T(2,128)}), f32[128,3,2,128]{3,2,1,0:T(2,128)S(1)}, u32[]{:S(2)}, u32[]{:S(2)}) %all-to-all-start) | async-done | bytes 393248 | tf_op jit(solution)/shard_map/all_to_all | solution.py:173
  37.5 0.0 copy-done.2
  37.5 0.7 copy-done
  38.2 7.4 %sweep.1 = f32[256,128]{1,0:T(8,128)} custom-call(s32[1]{0:T(128)} %bitcast.1.half_ref, f32[768,128]{1,0:T(8,128)} %bitcast.16, f32[8,128]{1,0:T(8,128)} %copy-done.1, f32[8,128]{1,0:T(8,128)} %copy-done.4, f32[8,128]{1,0:T(8,128)} %copy-done.3, f32[8,128]{1,0:T(8,128)} %copy-done.2), custom_call_target="tpu_custom_call" | custom-call | tf_op jit(solution)/shard_map/sweep/pallas_call | solution.py:175
  45.6 24.4 %all_to_all.10 = f32[128,2,128]{2,1,0:T(2,128)S(1)} all-to-all(f32[128,2,128]{2,1,0:T(2,128)} %bitcast.21), channel_id=1, replica_groups=mesh['band'=4,'tile'=16,'slab'=8] {'slab','tile'}, dimensions={0} | all-to-all | bytes 262144 | tf_op jit(solution)/shard_map/all_to_all | solution.py:189
  70.0 14.2 %all_gather.3.in_ref = f32[1024,128]{1,0:T(8,128)} all-gather(f32[256,128]{1,0:T(8,128)S(1)} %bitcast.22), channel_id=1, replica_groups=mesh['band'=4,'tile'=16,'slab'=8] {'band'}, dimensions={0}, use_global_device_ids=true | all-gather | bytes 655360 | tf_op jit(solution)/shard_map/all_gather | solution.py:190
  84.2 2.5 %finish.1 = (f32[5,128,64]{2,1,0:T(8,128)}, f32[8,128,256]{2,1,0:T(8,128)}) custom-call(s32[1]{0:T(128)} %bitcast.band_ref, s32[8]{0:T(128)} %line_ref.1, f32[1024,128]{1,0:T(8,128)} %all_gather.3.in_ref, f32[128,256]{1,0:T(8,128)} %bitcast.20), custom_call_target="tpu_custom_call" | custom-call | tf_op jit(solution)/shard_map/finish/pallas_call | solution.py:192
  (15 shorter events, 0.1 us)
Async XLA Ops:
  2.7 34.8 %all-to-all-start = ((f32[128,3,2,128]{3,2,1,0:T(2,128)}), f32[128,3,2,128]{3,2,1,0:T(2,128)S(1)}, u32[]{:S(2)}, u32[]{:S(2)}) async-start(f32[128,3,2,128]{3,2,1,0:T(2,128)} %bitcast.17), calls=%async_computation | async-start | bytes 786432 | tf_op jit(solution)/shard_map/all_to_all | solution.py:173
  20.1 0.7 copy-start.7
  20.8 0.7 copy-start.5
  21.4 0.7 copy-start.6
  22.2 10.2 %copy-start.1 = (f32[8,128]{1,0:T(8,128)}, f32[8,128]{1,0:T(8,128)S(1)}, u32[]{:S(2)}) copy-start(f32[8,128]{1,0:T(8,128)S(1)} %concatenate.3.refs_0_) | copy-start | bytes 12292
  22.2 10.2 %collective-permute-start.2 = (f32[8,128]{1,0:T(8,128)S(1)}, f32[8,128]{1,0:T(8,128)S(1)}, u32[]{:S(2)}, u32[]{:S(2)}) collective-permute-start(f32[8,128]{1,0:T(8,128)S(1)} %concatenate.3.refs_0_), channel_id=1, source_target_pairs={{0,384},{128,0},{256,128},{384,256},{1,385},{129,1},{257,129},{385... | collective-permute-start | bytes 12296 | tf_op jit(solution)/shard_map/ppermute | solution.py:152
  26.9 7.0 %collective-permute-start.1 = (f32[8,128]{1,0:T(8,128)S(1)}, f32[8,128]{1,0:T(8,128)S(1)}, u32[]{:S(2)}, u32[]{:S(2)}) collective-permute-start(f32[8,128]{1,0:T(8,128)S(1)} %concatenate.3.refs_0_), channel_id=1, source_target_pairs={{0,256},{128,384},{256,0},{384,128},{1,257},{129,385},{257,1},{385... | collective-permute-start | bytes 12296 | tf_op jit(solution)/shard_map/ppermute | solution.py:152
  29.6 6.7 %collective-permute-start = (f32[8,128]{1,0:T(8,128)S(1)}, f32[8,128]{1,0:T(8,128)S(1)}, u32[]{:S(2)}, u32[]{:S(2)}) collective-permute-start(f32[8,128]{1,0:T(8,128)S(1)} %concatenate.3.refs_0_), channel_id=1, source_target_pairs={{0,128},{128,256},{256,384},{384,0},{1,129},{129,257},{257,385},{3... | collective-permute-start | bytes 12296 | tf_op jit(solution)/shard_map/ppermute | solution.py:152
  32.5 5.0 %copy-start.2 = (f32[8,128]{1,0:T(8,128)}, f32[8,128]{1,0:T(8,128)S(1)}, u32[]{:S(2)}) copy-start(f32[8,128]{1,0:T(8,128)S(1)} %collective-permute-done.2.refs_3_) | copy-start | bytes 12292
  33.9 3.5 %copy-start.3 = (f32[8,128]{1,0:T(8,128)}, f32[8,128]{1,0:T(8,128)S(1)}, u32[]{:S(2)}) copy-start(f32[8,128]{1,0:T(8,128)S(1)} %collective-permute-done.1.refs_2_) | copy-start | bytes 12292
  36.4 1.1 %copy-start.4 = (f32[8,128]{1,0:T(8,128)}, f32[8,128]{1,0:T(8,128)S(1)}, u32[]{:S(2)}) copy-start(f32[8,128]{1,0:T(8,128)S(1)} %collective-permute-done.refs_1_) | copy-start | bytes 12292
  37.5 0.7 copy-start

commit v2 on v1

--- a/solution.py
+++ b/solution.py
@@ -3,6 +3,7 @@
 from jax import lax
 from jax.experimental import pallas as pl
 from jax.experimental.pallas import tpu as pltpu
+from jax.sharding import Mesh
 from jax.sharding import PartitionSpec as P
 
 LINES = 5
@@ -13,7 +14,7 @@
 LOG2E = 1.4426950408889634
 LANES = 128
 FIELDS = 6
-PLANE = ("slab", "tile")
+PLANE = ("yhi", "tile")
 
 
 def line_ratios(l1, l2, l3, l4):
@@ -26,7 +27,29 @@
     )
 
 
-def pack_kernel(band_ref, opacity_ref, planck_ref, levels_ref, out_ref, turned_ref):
+def pack_kernel(
+    band_ref,
+    opacity_ref,
+    planck_ref,
+    levels_ref,
+    strength_ref,
+    line_ref,
+    weight_ref,
+    out_ref,
+    params_ref,
+    turned_ref,
+):
+    shape = (8, LANES)
+    lane = lax.broadcasted_iota(jnp.int32, shape, 1) % 32 - band_ref[0] * 8
+    row = lax.broadcasted_iota(jnp.int32, shape, 0)
+    own = jnp.zeros(shape, jnp.float32)
+    for f in range(8):
+        weight = weight_ref[f] * (LINES / 64.0)
+        line = line_ref[f].astype(jnp.float32)
+        column = jnp.where(row == 0, strength_ref[f], jnp.where(row == 1, weight, jnp.where(row == 2, line, 0.0)))
+        own = jnp.where(lane == f, column, own)
+    for b in range(4):
+        params_ref[b] = own
     half = pl.multiple_of((band_ref[0] % 2) * 64, 64)
     inverse = 1.0 / levels_ref[0]
     fields = [opacity_ref[...], planck_ref[...]]
@@ -34,15 +57,11 @@
     for i, field in enumerate(fields):
         turned_ref[i] = field.T
         rows = turned_ref[i, pl.ds(half, 64), :]
-        out_ref[pl.ds(i, 64, stride=2 * FIELDS), :] = rows
-        out_ref[pl.ds(FIELDS + i, 64, stride=2 * FIELDS), :] = rows
-
-
-def sweep_kernel(half_ref, in_ref, *refs):
-    *param_refs, out_ref, w_ref, v_ref, y_ref, j_ref = refs
-    params = param_refs[0][...]
-    for ref in param_refs[1:]:
-        params = params + ref[...]
+        out_ref[pl.ds(i, 64, stride=FIELDS), :] = rows
+
+
+def sweep_kernel(core_ref, in_ref, params_ref, out_ref, w_ref, v_ref, y_ref, j_ref):
+    params = params_ref[0] + params_ref[1] + params_ref[2] + params_ref[3]
     decay = params[0:1] * (-PATH_FACTOR * LOG2E)
     weight = params[1:2]
     line = params[2:3].astype(jnp.int32)
@@ -69,10 +88,10 @@
     first_row, last_row = sub == 0, sub == 7
     lane8 = lax.broadcasted_iota(jnp.int32, (8, LANES), 1)
     inner_left, inner_right = lane8 >= 32, lane8 < 96
-    half = half_ref[0]
-
-    def slab(s, state):
-        base = s * 96
+    core = core_ref[0]
+
+    def slab(s, state, own):
+        base = pl.multiple_of((s % 2) * 384 + (s // 2) * 96, 96)
         op, pk, r1, r2, r3, r4 = [in_ref[pl.ds(base + i, 16, stride=FIELDS), :] for i in range(6)]
         sources = [EPS_THERMAL * pk + (1.0 - EPS_THERMAL) * q for q in line_ratios(r1, r2, r3, r4)]
         parts = jnp.concatenate([op, *sources], axis=0)
@@ -102,23 +121,33 @@
                     right[p] = a * ((1.0 - TILT_SHARE) * right[p] + TILT_SHARE * up_right[p]) + b
                     left[p] = a * ((1.0 - TILT_SHARE) * left[p] + TILT_SHARE * up_left[p]) + b
                     sums.append((right[p] + left[p]) * weight)
-                both = jnp.concatenate(sums, axis=0)
-                high = both.astype(jnp.bfloat16)
-                low = (both - high.astype(jnp.float32)).astype(jnp.bfloat16)
-                j_ref[z * 16 : z * 16 + 16, c * LANES : (c + 1) * LANES] = high
-                j_ref[z * 16 : z * 16 + 16, 512 + c * LANES : 512 + (c + 1) * LANES] = low
-        jbar = lax.dot_general(
-            v_ref[...], j_ref[...], (((1,), (1,)), ((), ())), preferred_element_type=jnp.float32
+                if own:
+                    both = jnp.concatenate(sums, axis=0)
+                    high = both.astype(jnp.bfloat16)
+                    low = (both - high.astype(jnp.float32)).astype(jnp.bfloat16)
+                    j_ref[z * 16 : z * 16 + 16, c * LANES : (c + 1) * LANES] = high
+                    j_ref[z * 16 : z * 16 + 16, 512 + c * LANES : 512 + (c + 1) * LANES] = low
+        if own:
+            jbar = lax.dot_general(
+                v_ref[...], j_ref[...], (((1,), (1,)), ((), ())), preferred_element_type=jnp.float32
+            )
+            jbar = [jbar[16 * t : 16 * t + 16] for t in range(LINES)]
+            ratio = [(j + COLLISION * pk) / (1.0 + j + COLLISION) for j in jbar]
+            level_1 = 0.5 * (ratio[0] / ratio[2] + ratio[1] / ratio[3])
+            level_2 = ratio[1] / ratio[4]
+            for k, level in enumerate((level_1, level_2, ratio[0], ratio[1])):
+                out_ref[pl.ds((s // 2) * 64 + k, 16, stride=4), :] = level
+        return tuple(right) + tuple(left)
+
+    def either(s, state):
+        return lax.cond(
+            s % 2 == core,
+            lambda state: slab(s, state, True),
+            lambda state: slab(s, state, False),
+            state,
         )
-        jbar = [jbar[16 * t : 16 * t + 16] for t in range(LINES)]
-        ratio = [(j + COLLISION * pk) / (1.0 + j + COLLISION) for j in jbar]
-        level_1 = 0.5 * (ratio[0] / ratio[2] + ratio[1] / ratio[3])
-        level_2 = ratio[1] / ratio[4]
-        out_ref[pl.ds(s * 32, 16, stride=2), :] = jnp.where(half == 0, level_1, ratio[0])
-        out_ref[pl.ds(s * 32 + 1, 16, stride=2), :] = jnp.where(half == 0, level_2, ratio[1])
-        return tuple(right) + tuple(left)
-
-    lax.fori_loop(0, 8, slab, (jnp.zeros((8, LANES), jnp.float32),) * 16)
+
+    lax.fori_loop(0, 8, either, (jnp.zeros((8, LANES), jnp.float32),) * 16)
 
 
 def finish_kernel(band_ref, line_ref, in_ref, planck_ref, levels_ref, source_ref, lines_ref):
@@ -141,19 +170,10 @@
     vmem = pl.BlockSpec(memory_space=pltpu.VMEM)
     smem = pl.BlockSpec(memory_space=pltpu.SMEM)
     band_1 = band.astype(jnp.int32).reshape(1)
-    half_1 = (lax.axis_index("tile") % 2).astype(jnp.int32).reshape(1)
-
-    own = jnp.stack([strength, line_weight * (LINES / 64.0), line_index.astype(jnp.float32)])
-    own = jnp.broadcast_to(own[:, None, None, :], (3, 4, 4, 8))
-    mine = (jnp.arange(4) == band)[None, None, :, None]
-    own = jnp.where(mine, own, 0.0).reshape(3, LANES)
-    own = jnp.concatenate([own, jnp.zeros((5, LANES), jnp.float32)], axis=0)
-    params = [own] + [
-        lax.ppermute(own, "band", [(i, (i + d) % 4) for i in range(4)]) for d in (1, 2, 3)
-    ]
+    core_1 = lax.axis_index("core").astype(jnp.int32).reshape(1)
 
     planck_2d = planck.reshape(128, 256)
-    packed = pl.pallas_call(
+    packed, own_params = pl.pallas_call(
         pack_kernel,
         grid_spec=pltpu.PrefetchScalarGridSpec(
             num_scalar_prefetch=1,
@@ -162,19 +182,38 @@
                 pl.BlockSpec((128, 128), lambda i, b: (0, b[0] // 2)),
                 pl.BlockSpec((128, 128), lambda i, b: (0, b[0] // 2)),
                 pl.BlockSpec((5, 128, 128), lambda i, b: (0, 0, b[0] // 2)),
+                smem,
+                smem,
+                smem,
             ],
-            out_specs=pl.BlockSpec((128 * FIELDS, LANES), lambda i, b: (0, 0)),
+            out_specs=[
+                pl.BlockSpec((64 * FIELDS, LANES), lambda i, b: (0, 0)),
+                pl.BlockSpec((4, 8, LANES), lambda i, b: (0, 0, 0)),
+            ],
             scratch_shapes=[pltpu.VMEM((FIELDS, 128, 128), jnp.float32)],
         ),
-        out_shape=jax.ShapeDtypeStruct((128 * FIELDS, LANES), jnp.float32),
+        out_shape=[
+            jax.ShapeDtypeStruct((64 * FIELDS, LANES), jnp.float32),
+            jax.ShapeDtypeStruct((4, 8, LANES), jnp.float32),
+        ],
         name="pack",
-    )(band_1, opacity.reshape(128, 256), planck_2d, old_populations.reshape(5, 128, 256))
-
-    plane = lax.all_to_all(packed.reshape(128, 3, 2, LANES), PLANE, 0, 0, tiled=True)
+    )(
+        band_1,
+        opacity.reshape(128, 256),
+        planck_2d,
+        old_populations.reshape(5, 128, 256),
+        strength,
+        line_index,
+        line_weight,
+    )
+
+    part = lax.all_to_all(packed.reshape(64, 3, 2, LANES), PLANE, 0, 0, tiled=True)
+    params = lax.all_to_all(own_params, "band", 0, 0, tiled=True)
+    plane = lax.all_gather(part.reshape(64 * FIELDS, LANES), "core", axis=0, tiled=True)
 
     swept = pl.pallas_call(
         sweep_kernel,
-        in_specs=[smem, vmem] + [vmem] * len(params),
+        in_specs=[smem, vmem, vmem],
         out_specs=vmem,
         out_shape=jax.ShapeDtypeStruct((256, LANES), jnp.float32),
         scratch_shapes=[
@@ -183,10 +222,11 @@
             pltpu.VMEM((128, 1024), jnp.float32),
             pltpu.VMEM((128, 1024), jnp.bfloat16),
         ],
+        compiler_params=pltpu.CompilerParams(vmem_limit_bytes=8 << 20),
         name="sweep",
-    )(half_1, plane.reshape(128 * FIELDS, LANES), *params)
-
-    quarter = lax.all_to_all(swept.reshape(128, 2, LANES), PLANE, 0, 0, tiled=True)
+    )(core_1, plane, params)
+
+    quarter = lax.all_to_all(swept.reshape(64, 4, LANES), PLANE, 0, 0, tiled=True)
     levels = lax.all_gather(quarter.reshape(256, LANES), "band", axis=0, tiled=True)
 
     new_levels, new_source = pl.pallas_call(
@@ -198,21 +238,25 @@
             jax.ShapeDtypeStruct((8, 128, 256), jnp.float32),
         ],
         scratch_shapes=[pltpu.VMEM((LINES, 128, 256), jnp.float32)],
+        compiler_params=pltpu.CompilerParams(vmem_limit_bytes=8 << 20),
         name="finish",
     )(band_1, line_index, levels, planck_2d)
     return new_levels.reshape(5, 8, 16, 64), new_source.reshape(8, 8, 16, 256)
 
 
 def solution(mesh):
+    bands, tiles, slabs = (mesh.shape[n] for n in ("band", "tile", "slab"))
+    fine = Mesh(mesh.devices.reshape(bands, tiles, slabs // 2, 2), ("band", "tile", "yhi", "core"))
+    slab = ("yhi", "core")
     in_specs = (
         P("band"),
-        P("slab", "tile", None),
-        P("slab", "tile", None),
-        P(None, "slab", "tile", None),
+        P(slab, "tile", None),
+        P(slab, "tile", None),
+        P(None, slab, "tile", None),
         P("band"),
         P("band"),
     )
-    out_specs = (P(None, "slab", "tile", "band"), P("band", "slab", "tile", None))
+    out_specs = (P(None, slab, "tile", "band"), P("band", slab, "tile", None))
     return jax.shard_map(
-        per_device, mesh=mesh, in_specs=in_specs, out_specs=out_specs, check_vma=False
-    )
+        per_device, mesh=fine, in_specs=in_specs, out_specs=out_specs, check_vma=False
+    )

time: 87 us -> 78.2 us (0.90)
  waiting for transfers between devices: 4.98 us -> 16 us
  blocking collectives: 38.6 us -> 31.9 us
  starting transfers between devices: 27.5 us -> 20.9 us
  Pallas kernels: 11.8 us -> 8.44 us
  local copies, waits for them, and re-layouts: 2.89 us -> 0.01 us
    all_to_all x1 -> x2, waiting for transfers between devices: 1.11 us -> 16 us  [the longest x1 12.7 us: per_device(): lax.all_to_all(packed.reshape(64, 3, 2, LANES), PLANE, 0, 0, tiled=True)]
    ppermute x3 -> x0, starting transfers between devices: 10.2 us -> none  [per_device(): lax.ppermute(own, 'band', [(i, (i + d) % 4) for i in range(4)])]
    all_to_all x1, blocking collectives: 24.4 us -> 16.7 us  [per_device(): lax.all_to_all(swept.reshape(64, 4, LANES), PLANE, 0, 0, tiled=True)]
    ppermute x3 -> x0, waiting for transfers between devices: 3.88 us -> none  [per_device(): lax.ppermute(own, 'band', [(i, (i + d) % 4) for i in range(4)])]
    all_to_all x1 -> x2, starting transfers between devices: 17.4 us -> 20.9 us  [the longest x1 16.6 us: per_device(): lax.all_to_all(packed.reshape(64, 3, 2, LANES), PLANE, 0, 0, tiled=True)]
    pallas_call x1, Pallas kernels: 7.37 us -> 4.55 us  [per_device(): pl.pallas_call(sweep_kernel, in_specs=[smem, vmem, vmem], out_specs=vmem,...]
    unnamed x16 -> x4, local copies, waits for them, and re-layouts: 2.62 us -> 0.01 us
    all_gather x0 -> x1, blocking collectives: none -> 2.07 us  [per_device(): lax.all_gather(part.reshape(64 * FIELDS, LANES), 'core', axis=0, tiled=True)]
  transfers between devices with their start and end apart: 4 -> 2, of which waited for: 3 -> 2; matrix products, arithmetic and copies ran while one was open for 0% -> 0% of each run, Pallas kernels for 0% -> 0%
where the time goes in v2:
time: 78.2 us; the launch traced here: 77.9 us
  blocking collectives  31.9 us (41%)
  starting transfers between devices  20.9 us (27%)
  waiting for transfers between devices  16 us (20%)
  Pallas kernels  8.44 us (11%)
    all_to_all x1, blocking collectives, per_device(): lax.all_to_all(swept.reshape(64, 4, LANES), PLANE, 0, 0, tiled=True)  16.7 us
    all_to_all x1, starting transfers between devices, per_device(): lax.all_to_all(packed.reshape(64, 3, 2, LANES), PLANE, 0, 0, tiled=True)  16.6 us
    all_gather x1, blocking collectives, per_device(): lax.all_gather(quarter.reshape(256, LANES), 'band', axis=0, tiled=True)  13.1 us
    all_to_all x1, waiting for transfers between devices, per_device(): lax.all_to_all(packed.reshape(64, 3, 2, LANES), PLANE, 0, 0, tiled=True)  12.7 us
    pallas_call x1, Pallas kernels, per_device(): pl.pallas_call(sweep_kernel, in_specs=[smem, vmem, vmem], out_specs=vmem,...  4.55 us
    all_to_all x1, starting transfers between devices, per_device(): params = lax.all_to_all(own_params, 'band', 0, 0, tiled=True)  4.29 us
    all_to_all x1, waiting for transfers between devices, per_device(): params = lax.all_to_all(own_params, 'band', 0, 0, tiled=True)  3.29 us
    all_gather x1, blocking collectives, per_device(): lax.all_gather(part.reshape(64 * FIELDS, LANES), 'core', axis=0, tiled=True)  2.07 us
  transfers between devices with their start and end apart: 2, of which 2 were waited for; matrix products, arithmetic and copies ran while one was open for 0% of the time, Pallas kernels for 0%

profile of v2, /device:TPU:8, one launch (start us, length us, event | category | flops | bytes accessed | tf_op | source)
XLA Modules:
  0.0 77.9 jit_solution(4648160309564298673)
XLA Ops:
  0.6 2.0 %pack.1 = (f32[384,128]{1,0:T(8,128)}, f32[4,8,128]{2,1,0:T(8,128)}) custom-call(s32[1]{0:T(128)} %bitcast.band_ref, f32[128,256]{1,0:T(8,128)} %bitcast.18, f32[128,256]{1,0:T(8,128)} %bitcast.11, f32[5,128,256]{2,1,0:T(8,128)} %bitcast.15, f32[8]{0:T(128)} %strength_ref.1, s32[8]{0:T(128)} %line_ref.3, f32[8]{0:T(128)} %weight_ref.1), custom_call_target="tpu_custom_call" | custom-call | tf_op jit(solution)/shard_map/pack/pallas_call | solution.py:176
  2.6 16.6 %all-to-all-start = ((f32[64,3,2,128]{3,2,1,0:T(2,128)}), f32[64,3,2,128]{3,2,1,0:T(2,128)S(1)}, u32[]{:S(2)}, u32[]{:S(2)}) async-start(f32[64,3,2,128]{3,2,1,0:T(2,128)} %bitcast.17), calls=%async_computation | async-start | bytes 393216 | tf_op jit(solution)/shard_map/all_to_all | solution.py:210
  19.2 12.7 %all-to-all-done = f32[64,3,2,128]{3,2,1,0:T(2,128)S(1)} async-done(((f32[64,3,2,128]{3,2,1,0:T(2,128)}), f32[64,3,2,128]{3,2,1,0:T(2,128)S(1)}, u32[]{:S(2)}, u32[]{:S(2)}) %all-to-all-start) | async-done | bytes 196640 | tf_op jit(solution)/shard_map/all_to_all | solution.py:210
  31.9 4.3 %all-to-all-start.1 = ((f32[4,8,128]{2,1,0:T(8,128)}), f32[4,8,128]{2,1,0:T(8,128)S(1)}, u32[]{:S(2)}, u32[]{:S(2)}) async-start(f32[4,8,128]{2,1,0:T(8,128)} %get-tuple-element.7), calls=%async_computation.1 | async-start | bytes 32768 | tf_op jit(solution)/shard_map/all_to_all | solution.py:211
  36.2 2.1 %all_gather.6.in_ref = f32[768,128]{1,0:T(8,128)S(1)} all-gather(f32[384,128]{1,0:T(8,128)S(1)} %bitcast.14), channel_id=1, replica_groups=mesh['band'=4,'tile'=16,'yhi'=4,'core'=2] {'core'}, dimensions={0}, use_global_device_ids=true | all-gather | bytes 589824 | tf_op jit(solution)/shard_map/all_gather | solution.py:212
  38.2 3.3 %all-to-all-done.1.params_ref = f32[4,8,128]{2,1,0:T(8,128)S(1)} async-done(((f32[4,8,128]{2,1,0:T(8,128)}), f32[4,8,128]{2,1,0:T(8,128)S(1)}, u32[]{:S(2)}, u32[]{:S(2)}) %all-to-all-start.1) | async-done | bytes 16416 | tf_op jit(solution)/shard_map/all_to_all | solution.py:211
  41.5 4.5 %sweep.1 = f32[256,128]{1,0:T(8,128)S(1)} custom-call(s32[1]{0:T(128)} %bitcast.1.core_ref, f32[768,128]{1,0:T(8,128)S(1)} %all_gather.6.in_ref, f32[4,8,128]{2,1,0:T(8,128)S(1)} %all-to-all-done.1.params_ref), custom_call_target="tpu_custom_call" | custom-call | tf_op jit(solution)/shard_map/sweep/pallas_call | solution.py:214
  46.1 16.7 %all_to_all.15 = f32[64,4,128]{2,1,0:T(4,128)S(1)} all-to-all(f32[64,4,128]{2,1,0:T(4,128)S(1)} %bitcast.13), channel_id=1, replica_groups=mesh['band'=4,'tile'=16,'yhi'=4,'core'=2] {'yhi','tile'}, dimensions={0} | all-to-all | bytes 262144 | tf_op jit(solution)/shard_map/all_to_all | solution.py:229
  62.8 0.0 copy-start
  62.8 0.0 copy-start.1
  62.8 13.1 %all_gather.7.in_ref = f32[1024,128]{1,0:T(8,128)S(1)} all-gather(f32[256,128]{1,0:T(8,128)S(1)} %bitcast.16), channel_id=1, replica_groups=mesh['band'=4,'tile'=16,'yhi'=4,'core'=2] {'band'}, dimensions={0}, use_global_device_ids=true | all-gather | bytes 655360 | tf_op jit(solution)/shard_map/all_gather | solution.py:230
  75.9 0.0 copy-done
  75.9 0.0 copy-done.1
  75.9 1.9 %finish.1 = (f32[5,128,64]{2,1,0:T(8,128)}, f32[8,128,256]{2,1,0:T(8,128)}) custom-call(s32[1]{0:T(128)} %bitcast.band_ref, s32[8]{0:T(128)S(1)} %copy-done.1, f32[1024,128]{1,0:T(8,128)S(1)} %all_gather.7.in_ref, f32[128,256]{1,0:T(8,128)S(1)} %bitcast.12), custom_call_target="tpu_custom_call" | custom-call | tf_op jit(solution)/shard_map/finish/pallas_call | solution.py:232
Async XLA Ops:
  2.6 29.3 %all-to-all-start = ((f32[64,3,2,128]{3,2,1,0:T(2,128)}), f32[64,3,2,128]{3,2,1,0:T(2,128)S(1)}, u32[]{:S(2)}, u32[]{:S(2)}) async-start(f32[64,3,2,128]{3,2,1,0:T(2,128)} %bitcast.17), calls=%async_computation | async-start | bytes 393216 | tf_op jit(solution)/shard_map/all_to_all | solution.py:210
  31.9 9.7 %all-to-all-start.1 = ((f32[4,8,128]{2,1,0:T(8,128)}), f32[4,8,128]{2,1,0:T(8,128)S(1)}, u32[]{:S(2)}, u32[]{:S(2)}) async-start(f32[4,8,128]{2,1,0:T(8,128)} %get-tuple-element.7), calls=%async_computation.1 | async-start | bytes 32768 | tf_op jit(solution)/shard_map/all_to_all | solution.py:211
  62.8 13.1 %copy-start = (f32[8,16,256]{2,1,0:T(8,128)S(1)}, f32[8,16,256]{2,1,0:T(8,128)}, u32[]{:S(2)}) copy-start(f32[8,16,256]{2,1,0:T(8,128)} %param.8) | copy-start | bytes 393220
  62.8 13.1 %copy-start.1 = (s32[8]{0:T(128)S(1)}, s32[8]{0:T(128)}, u32[]{:S(2)}) copy-start(s32[8]{0:T(128)} %line_ref.3) | copy-start | bytes 100

commit v3 on v2

--- a/solution.py
+++ b/solution.py
@@ -48,8 +48,7 @@
         line = line_ref[f].astype(jnp.float32)
         column = jnp.where(row == 0, strength_ref[f], jnp.where(row == 1, weight, jnp.where(row == 2, line, 0.0)))
         own = jnp.where(lane == f, column, own)
-    for b in range(4):
-        params_ref[b] = own
+    params_ref[...] = own
     half = pl.multiple_of((band_ref[0] % 2) * 64, 64)
     inverse = 1.0 / levels_ref[0]
     fields = [opacity_ref[...], planck_ref[...]]
@@ -60,8 +59,8 @@
         out_ref[pl.ds(i, 64, stride=FIELDS), :] = rows
 
 
-def sweep_kernel(core_ref, in_ref, params_ref, out_ref, w_ref, v_ref, y_ref, j_ref):
-    params = params_ref[0] + params_ref[1] + params_ref[2] + params_ref[3]
+def sweep_kernel(core_ref, in_ref, params_ref, out_ref, w_ref, v_ref, even_ref, odd_ref, j_ref):
+    params = params_ref[...]
     decay = params[0:1] * (-PATH_FACTOR * LOG2E)
     weight = params[1:2]
     line = params[2:3].astype(jnp.int32)
@@ -90,9 +89,12 @@
     inner_left, inner_right = lane8 >= 32, lane8 < 96
     core = core_ref[0]
 
-    def slab(s, state, own):
+    def fields(s):
         base = pl.multiple_of((s % 2) * 384 + (s // 2) * 96, 96)
-        op, pk, r1, r2, r3, r4 = [in_ref[pl.ds(base + i, 16, stride=FIELDS), :] for i in range(6)]
+        return [in_ref[pl.ds(base + i, 16, stride=FIELDS), :] for i in range(6)]
+
+    def spread(s, y_ref):
+        op, pk, r1, r2, r3, r4 = fields(s)
         sources = [EPS_THERMAL * pk + (1.0 - EPS_THERMAL) * q for q in line_ratios(r1, r2, r3, r4)]
         parts = jnp.concatenate([op, *sources], axis=0)
         high = parts.astype(jnp.bfloat16)
@@ -103,6 +105,8 @@
             (((0,), (0,)), ((), ())),
             preferred_element_type=jnp.float32,
         )
+
+    def slab(s, state, y_ref, own):
         right, left = list(state[:8]), list(state[8:])
         for z in range(8):
             turned = [pltpu.roll(v, 1, 0) for v in right]
@@ -127,27 +131,50 @@
                     low = (both - high.astype(jnp.float32)).astype(jnp.bfloat16)
                     j_ref[z * 16 : z * 16 + 16, c * LANES : (c + 1) * LANES] = high
                     j_ref[z * 16 : z * 16 + 16, 512 + c * LANES : 512 + (c + 1) * LANES] = low
-        if own:
-            jbar = lax.dot_general(
-                v_ref[...], j_ref[...], (((1,), (1,)), ((), ())), preferred_element_type=jnp.float32
-            )
-            jbar = [jbar[16 * t : 16 * t + 16] for t in range(LINES)]
-            ratio = [(j + COLLISION * pk) / (1.0 + j + COLLISION) for j in jbar]
-            level_1 = 0.5 * (ratio[0] / ratio[2] + ratio[1] / ratio[3])
-            level_2 = ratio[1] / ratio[4]
-            for k, level in enumerate((level_1, level_2, ratio[0], ratio[1])):
-                out_ref[pl.ds((s // 2) * 64 + k, 16, stride=4), :] = level
         return tuple(right) + tuple(left)
 
-    def either(s, state):
-        return lax.cond(
-            s % 2 == core,
-            lambda state: slab(s, state, True),
-            lambda state: slab(s, state, False),
-            state,
+    def relax(s):
+        pk = fields(s)[1]
+        jbar = lax.dot_general(
+            v_ref[...], j_ref[...], (((1,), (1,)), ((), ())), preferred_element_type=jnp.float32
         )
-
-    lax.fori_loop(0, 8, either, (jnp.zeros((8, LANES), jnp.float32),) * 16)
+        jbar = [jbar[16 * t : 16 * t + 16] for t in range(LINES)]
+        ratio = [(j + COLLISION * pk) / (1.0 + j + COLLISION) for j in jbar]
+        level_1 = 0.5 * (ratio[0] / ratio[2] + ratio[1] / ratio[3])
+        level_2 = ratio[1] / ratio[4]
+        for k, level in enumerate((level_1, level_2, ratio[0], ratio[1])):
+            out_ref[pl.ds((s // 2) * 64 + k, 16, stride=4), :] = level
+
+    def sweep_even():
+        def two_slabs(i, state):
+            spread(2 * i + 1, odd_ref)
+            state = slab(2 * i, state, even_ref, True)
+            relax(2 * i)
+            spread(2 * i + 2, even_ref)
+            return slab(2 * i + 1, state, odd_ref, False)
+
+        spread(0, even_ref)
+        state = lax.fori_loop(0, 3, two_slabs, start)
+        slab(6, state, even_ref, True)
+        relax(6)
+
+    def sweep_odd():
+        def two_slabs(i, state):
+            spread(2 * i + 2, even_ref)
+            state = slab(2 * i + 1, state, odd_ref, True)
+            relax(2 * i + 1)
+            spread(2 * i + 3, odd_ref)
+            return slab(2 * i + 2, state, even_ref, False)
+
+        spread(0, even_ref)
+        spread(1, odd_ref)
+        state = lax.fori_loop(0, 3, two_slabs, slab(0, start, even_ref, False))
+        slab(7, state, odd_ref, True)
+        relax(7)
+
+    start = (jnp.zeros((8, LANES), jnp.float32),) * 16
+    pl.when(core == 0)(sweep_even)
+    pl.when(core == 1)(sweep_odd)
 
 
 def finish_kernel(band_ref, line_ref, in_ref, planck_ref, levels_ref, source_ref, lines_ref):
@@ -188,13 +215,13 @@
             ],
             out_specs=[
                 pl.BlockSpec((64 * FIELDS, LANES), lambda i, b: (0, 0)),
-                pl.BlockSpec((4, 8, LANES), lambda i, b: (0, 0, 0)),
+                pl.BlockSpec((8, LANES), lambda i, b: (0, 0)),
             ],
             scratch_shapes=[pltpu.VMEM((FIELDS, 128, 128), jnp.float32)],
         ),
         out_shape=[
             jax.ShapeDtypeStruct((64 * FIELDS, LANES), jnp.float32),
-            jax.ShapeDtypeStruct((4, 8, LANES), jnp.float32),
+            jax.ShapeDtypeStruct((8, LANES), jnp.float32),
         ],
         name="pack",
     )(
@@ -208,7 +235,7 @@
     )
 
     part = lax.all_to_all(packed.reshape(64, 3, 2, LANES), PLANE, 0, 0, tiled=True)
-    params = lax.all_to_all(own_params, "band", 0, 0, tiled=True)
+    params = lax.psum(own_params, "band")
     plane = lax.all_gather(part.reshape(64 * FIELDS, LANES), "core", axis=0, tiled=True)
 
     swept = pl.pallas_call(
@@ -219,6 +246,7 @@
         scratch_shapes=[
             pltpu.VMEM((192, 1024), jnp.bfloat16),
             pltpu.VMEM((80, 1024), jnp.bfloat16),
+            pltpu.VMEM((128, 1024), jnp.float32),
             pltpu.VMEM((128, 1024), jnp.float32),
             pltpu.VMEM((128, 1024), jnp.bfloat16),
         ],

time: 78.2 us -> 74.8 us (0.957)
  blocking collectives: 31.9 us -> 48.6 us
  waiting for transfers between devices: 16 us -> 1.52 us
  starting transfers between devices: 20.9 us -> 16.6 us
  Pallas kernels: 8.44 us -> 6.42 us
    all_to_all x1, waiting for transfers between devices: 12.7 us -> 1.52 us  [per_device(): lax.all_to_all(packed.reshape(64, 3, 2, LANES), PLANE, 0, 0, tiled=True)]
    psum x0 -> x1, blocking collectives: none -> 10.5 us  [per_device(): params = lax.psum(own_params, 'band')]
    all_to_all x1, blocking collectives: 16.7 us -> 23.1 us  [per_device(): lax.all_to_all(swept.reshape(64, 4, LANES), PLANE, 0, 0, tiled=True)]
    all_to_all x1 -> x0, starting transfers between devices: 4.29 us -> none  [per_device(): params = lax.all_to_all(own_params, 'band', 0, 0, tiled=True)]
    all_to_all x1 -> x0, waiting for transfers between devices: 3.29 us -> none  [per_device(): params = lax.all_to_all(own_params, 'band', 0, 0, tiled=True)]
    pallas_call x1, Pallas kernels: 4.55 us -> 2.53 us  [per_device(): pl.pallas_call(sweep_kernel, in_specs=[smem, vmem, vmem], out_specs=vmem,...]
  transfers between devices with their start and end apart: 2 -> 1, of which waited for: 2 -> 1; matrix products, arithmetic and copies ran while one was open for 0% -> 0% of each run, Pallas kernels for 0% -> 0%
where the time goes in v3:
time: 74.8 us; the launch traced here: 74.5 us
  blocking collectives  48.6 us (65%)
  starting transfers between devices  16.6 us (22%)
  Pallas kernels  6.42 us (9%)
  waiting for transfers between devices  1.52 us (2%)
    all_to_all x1, blocking collectives, per_device(): lax.all_to_all(swept.reshape(64, 4, LANES), PLANE, 0, 0, tiled=True)  23.1 us
    all_to_all x1, starting transfers between devices, per_device(): lax.all_to_all(packed.reshape(64, 3, 2, LANES), PLANE, 0, 0, tiled=True)  16.6 us
    all_gather x1, blocking collectives, per_device(): lax.all_gather(quarter.reshape(256, LANES), 'band', axis=0, tiled=True)  12.9 us
    psum x1, blocking collectives, per_device(): params = lax.psum(own_params, 'band')  10.5 us
    pallas_call x1, Pallas kernels, per_device(): pl.pallas_call(sweep_kernel, in_specs=[smem, vmem, vmem], out_specs=vmem,...  2.53 us
    all_gather x1, blocking collectives, per_device(): lax.all_gather(part.reshape(64 * FIELDS, LANES), 'core', axis=0, tiled=True)  2.08 us
    pallas_call x1, Pallas kernels, per_device(): pl.pallas_call(pack_kernel, grid_spec=pltpu.PrefetchScalarGridSpec(num_sc...  1.96 us
    pallas_call x1, Pallas kernels, per_device(): pl.pallas_call(finish_kernel, in_specs=[smem, smem, vmem, vmem], out_spec...  1.93 us
  transfers between devices with their start and end apart: 1, of which 1 were waited for; matrix products, arithmetic and copies ran while one was open for 0% of the time, Pallas kernels for 0%

profile of v3, /device:TPU:8, one launch (start us, length us, event | category | flops | bytes accessed | tf_op | source)
XLA Modules:
  0.0 74.5 jit_solution(11399141364316779720)
XLA Ops:
  0.6 2.0 %pack.1 = (f32[384,128]{1,0:T(8,128)}, f32[8,128]{1,0:T(8,128)}) custom-call(s32[1]{0:T(128)} %bitcast.band_ref, f32[128,256]{1,0:T(8,128)} %bitcast.18, f32[128,256]{1,0:T(8,128)} %bitcast.11, f32[5,128,256]{2,1,0:T(8,128)} %bitcast.15, f32[8]{0:T(128)} %strength_ref.1, s32[8]{0:T(128)} %line_ref.3, f32[8]{0:T(128)} %weight_ref.1), custom_call_target="tpu_custom_call" | custom-call | tf_op jit(solution)/shard_map/pack/pallas_call | solution.py:203
  2.6 16.6 %all-to-all-start = ((f32[64,3,2,128]{3,2,1,0:T(2,128)}), f32[64,3,2,128]{3,2,1,0:T(2,128)S(1)}, u32[]{:S(2)}, u32[]{:S(2)}) async-start(f32[64,3,2,128]{3,2,1,0:T(2,128)} %bitcast.17), calls=%async_computation | async-start | bytes 393216 | tf_op jit(solution)/shard_map/all_to_all | solution.py:237
  19.2 0.0 copy-start.2
  19.2 0.7 copy-done.2
  19.9 10.5 %psum.7.params_ref = f32[8,128]{1,0:T(8,128)S(1)} all-reduce(f32[8,128]{1,0:T(8,128)S(1)} %copy-done.2), channel_id=1, replica_groups=mesh['band'=4,'tile'=16,'yhi'=4,'core'=2] {'band'}, use_global_device_ids=true, to_apply=%region_0.0 | all-reduce | flops 1024 | bytes 8192 | tf_op jit(solution)/shard_map/psum | solution.py:238
  30.3 1.5 %all-to-all-done = f32[64,3,2,128]{3,2,1,0:T(2,128)S(1)} async-done(((f32[64,3,2,128]{3,2,1,0:T(2,128)}), f32[64,3,2,128]{3,2,1,0:T(2,128)S(1)}, u32[]{:S(2)}, u32[]{:S(2)}) %all-to-all-start) | async-done | bytes 196640 | tf_op jit(solution)/shard_map/all_to_all | solution.py:237
  31.9 2.1 %all_gather.6.in_ref = f32[768,128]{1,0:T(8,128)S(1)} all-gather(f32[384,128]{1,0:T(8,128)S(1)} %bitcast.14), channel_id=1, replica_groups=mesh['band'=4,'tile'=16,'yhi'=4,'core'=2] {'core'}, dimensions={0}, use_global_device_ids=true | all-gather | bytes 589824 | tf_op jit(solution)/shard_map/all_gather | solution.py:239
  33.9 2.5 %sweep.1 = f32[256,128]{1,0:T(8,128)S(1)} custom-call(s32[1]{0:T(128)} %bitcast.1.core_ref, f32[768,128]{1,0:T(8,128)S(1)} %all_gather.6.in_ref, f32[8,128]{1,0:T(8,128)S(1)} %psum.7.params_ref), custom_call_target="tpu_custom_call" | custom-call | tf_op jit(solution)/shard_map/sweep/pallas_call | solution.py:241
  36.5 23.1 %all_to_all.10 = f32[64,4,128]{2,1,0:T(4,128)S(1)} all-to-all(f32[64,4,128]{2,1,0:T(4,128)S(1)} %bitcast.13), channel_id=1, replica_groups=mesh['band'=4,'tile'=16,'yhi'=4,'core'=2] {'yhi','tile'}, dimensions={0} | all-to-all | bytes 262144 | tf_op jit(solution)/shard_map/all_to_all | solution.py:257
  59.6 0.0 copy-start
  59.6 0.0 copy-start.1
  59.6 12.9 %all_gather.7.in_ref = f32[1024,128]{1,0:T(8,128)S(1)} all-gather(f32[256,128]{1,0:T(8,128)S(1)} %bitcast.16), channel_id=1, replica_groups=mesh['band'=4,'tile'=16,'yhi'=4,'core'=2] {'band'}, dimensions={0}, use_global_device_ids=true | all-gather | bytes 655360 | tf_op jit(solution)/shard_map/all_gather | solution.py:258
  72.5 0.0 copy-done
  72.5 0.0 copy-done.1
  72.5 1.9 %finish.1 = (f32[5,128,64]{2,1,0:T(8,128)}, f32[8,128,256]{2,1,0:T(8,128)}) custom-call(s32[1]{0:T(128)} %bitcast.band_ref, s32[8]{0:T(128)S(1)} %copy-done.1, f32[1024,128]{1,0:T(8,128)S(1)} %all_gather.7.in_ref, f32[128,256]{1,0:T(8,128)S(1)} %bitcast.12), custom_call_target="tpu_custom_call" | custom-call | tf_op jit(solution)/shard_map/finish/pallas_call | solution.py:260
Async XLA Ops:
  2.6 29.3 %all-to-all-start = ((f32[64,3,2,128]{3,2,1,0:T(2,128)}), f32[64,3,2,128]{3,2,1,0:T(2,128)S(1)}, u32[]{:S(2)}, u32[]{:S(2)}) async-start(f32[64,3,2,128]{3,2,1,0:T(2,128)} %bitcast.17), calls=%async_computation | async-start | bytes 393216 | tf_op jit(solution)/shard_map/all_to_all | solution.py:237
  19.2 0.7 copy-start.2
  59.6 12.9 %copy-start = (f32[8,16,256]{2,1,0:T(8,128)S(1)}, f32[8,16,256]{2,1,0:T(8,128)}, u32[]{:S(2)}) copy-start(f32[8,16,256]{2,1,0:T(8,128)} %param.8) | copy-start | bytes 393220
  59.6 12.9 %copy-start.1 = (s32[8]{0:T(128)S(1)}, s32[8]{0:T(128)}, u32[]{:S(2)}) copy-start(s32[8]{0:T(128)} %line_ref.3) | copy-start | bytes 100
